TPU v7x, 128 devices: a whole 4x4x4 slice. The times are simulated.
128 devices in a mesh: ma: 4 (over y), mb: 32 (over x, z, core).
Axes of the slice: x: 4, y: 4, z: 4, core: 2. Of those that a mesh axis runs over, the one named last changes fastest.
Arguments:
- tier_four: float32 [1024, 2, 128, 128], P(('ma', 'mb')), may hold values from -6 to 6
- tier_six: float32 [1024, 2, 128, 128], P(('ma', 'mb')), may hold values from -6 to 6
- tier_seven: float32 [1024, 2, 128, 128], P(('ma', 'mb')), may hold values from -6 to 6
- coupling: float32 [128, 128], replicated
- eigenbasis: float32 [128, 128], replicated
- energies: float32 [128], replicated, may hold values from -6 to 6
- decay_rates: float32 [12], replicated, may hold values from 0.5 to 4
- bath_coefficients: float32 [2, 12], replicated, may hold values from -1 to 1
- occupation_five: int32 [1024, 12], P(('ma', 'mb')), may hold values from 0 to 5, as said below
- local_five: int32 [1024, 2, 9], P(('ma', 'mb')), may hold values from 0 to 7
- peers_five: int32 [1024, 4], P(('ma', 'mb')), may hold values from 0 to 31, all different within a row; in each aligned block of 8 rows (0 to 7, 8 to 15, ...) at most 2 rows name the same one
- places_five: int32 [1024, 4], P(('ma', 'mb')), may hold values from 0 to 7
- occupation_six: int32 [1024, 12], P(('ma', 'mb')), may hold values from 0 to 6, as said below
- local_six: int32 [1024, 2, 9], P(('ma', 'mb')), may hold values from 0 to 7
- peers_six: int32 [1024, 4], P(('ma', 'mb')), may hold values from 0 to 31, all different within a row; in each aligned block of 8 rows (0 to 7, 8 to 15, ...) at most 2 rows name the same one
- places_six: int32 [1024, 4], P(('ma', 'mb')), may hold values from 0 to 7
Outputs:
- updated_five: float32 [1024, 2, 128, 128], P(('ma', 'mb'))
- updated_six: float32 [1024, 2, 128, 128], P(('ma', 'mb'))
Inputs may be any that keep to these rules, and one draw needn't show every extreme that they name: `occupation_five`: each row sums to 5; the first row of every block of 8 rows has all 5 in one mode. `occupation_six`: each row sums to 6; the first row of every block of 8 rows has all 6 in one mode. `local_five`: positions within the matrix's own block of 8 rows; a lowered entry is read only where its mode's occupation is positive. `local_six`: positions within the matrix's own block of 8 rows; a lowered entry is read only where its mode's occupation is positive. `peers_five`: the four entries of a row differ; among the rows of one block of 8 rows no value appears more than 2 times, and some value appears exactly 2 times. `peers_six`: the four entries of a row differ; among the rows of one block of 8 rows no value appears more than 2 times, and some value appears exactly 2 times.
All inputs are finite; a program needn't handle non-finite values.
Results may differ from a plain program's by a relative error of at most 0.0003.
Values sent between devices are 32-bit elements; how exact they have to be, the bound alone decides.
A program may use at most 128 MiB of HBM per device.

v0:
```python
import jax
import jax.numpy as jnp
from jax import lax
from jax.sharding import PartitionSpec as P

HIGHEST = lax.Precision.HIGHEST


def passed_along(array, axis, by):
    peers = lax.axis_size(axis)
    return lax.ppermute(array, axis, [(i, (i + by) % peers) for i in range(peers)])


def left_product(matrix, batch):
    return jnp.einsum("ij,mjk->mik", matrix, batch, precision=HIGHEST)


def right_product(batch, matrix):
    return jnp.einsum("mij,jk->mik", batch, matrix, precision=HIGHEST)


def mix_terms(up_real, up_imag, sum_rr, sum_ri, sum_ir, sum_ii):
    return (
        up_real + sum_rr - sum_ii,
        up_imag + sum_ri + sum_ir,
        up_real + sum_rr + sum_ii,
        up_imag + sum_ri - sum_ir,
    )


def settle(
    pair_real,
    pair_imag,
    other_real,
    other_imag,
    occupation,
    coupling,
    eigenbasis,
    energies,
    decay_rates,
):
    comm_real = left_product(coupling, pair_real) - right_product(other_real, coupling)
    comm_imag = left_product(coupling, pair_imag) - right_product(other_imag, coupling)
    turned = jnp.transpose(eigenbasis)
    eigen_real = right_product(left_product(turned, -comm_imag), eigenbasis)
    eigen_imag = right_product(left_product(turned, comm_real), eigenbasis)
    damping = jnp.dot(occupation.astype(jnp.float32), decay_rates, precision=HIGHEST)[:, None, None]
    splitting = (energies[:, None] - energies[None, :])[None]
    denominator = damping * damping + splitting * splitting
    factor_real = -damping / denominator
    factor_imag = splitting / denominator
    solved_real = eigen_real * factor_real - eigen_imag * factor_imag
    solved_imag = eigen_real * factor_imag + eigen_imag * factor_real
    back_real = right_product(left_product(eigenbasis, solved_real), turned)
    back_imag = right_product(left_product(eigenbasis, solved_imag), turned)
    return jnp.stack([back_real, back_imag], axis=1)


def first_mode(lower_tier, upper_tier):
    raised_first = passed_along(upper_tier, "ma", -1)
    lowered_first = passed_along(lower_tier, "ma", 1)
    return (raised_first, lowered_first)


def request_table(peer_ids, wanted, capacity, peer_count):
    onehot = (peer_ids[:, None] == jnp.arange(peer_count, dtype=jnp.int32)[None, :]).astype(
        jnp.int32
    )
    ranking = jnp.cumsum(onehot, axis=0) - 1
    placed = peer_ids * capacity + jnp.sum(ranking * onehot, axis=1)
    table = jnp.zeros((peer_count * capacity,), jnp.int32).at[placed].set(wanted)
    return (table.reshape(peer_count, capacity), placed)


def fetch_plain(table, store):
    return lax.all_to_all(
        store[lax.all_to_all(table, "mb", split_axis=0, concat_axis=0, tiled=True)],
        "mb",
        split_axis=0,
        concat_axis=0,
        tiled=True,
    )


def pick_rows(received, placed):
    flat_rows = received.reshape((-1,) + received.shape[2:])
    return flat_rows[placed]


def combine(
    lower_tier,
    upper_tier,
    raised_first,
    lowered_first,
    remote,
    nearby,
    occupation,
    bath_coefficients,
):
    count_rows = lower_tier.shape[0]
    shape_tail = lower_tier.shape[2:]
    spots = jnp.arange(count_rows, dtype=jnp.int32)
    counted = occupation.astype(jnp.float32)
    weight_real = counted * bath_coefficients[0][None, :]
    weight_imag = counted * bath_coefficients[1][None, :]
    up_hits = jnp.sum((nearby[:, 0, :, None] == spots[None, None, :]).astype(jnp.float32), axis=1)
    down_hits = (nearby[:, 1, :, None] == spots[None, None, :]).astype(jnp.float32)
    local_real = jnp.einsum("mk,mkj->mj", weight_real[:, 3:], down_hits, precision=HIGHEST)
    local_imag = jnp.einsum("mk,mkj->mj", weight_imag[:, 3:], down_hits, precision=HIGHEST)
    flat_upper = upper_tier.reshape(count_rows, -1)
    up_sum = jnp.dot(up_hits, flat_upper, precision=HIGHEST).reshape(upper_tier.shape)
    up_sum = up_sum + raised_first + remote[:, 0] + remote[:, 1]
    edges = jnp.stack([lowered_first, remote[:, 2], remote[:, 3]], axis=1)

    def weighted(local_weights, edge_weights, part_index):
        flat_part = lower_tier[:, part_index].reshape(count_rows, -1)
        inner = jnp.dot(local_weights, flat_part, precision=HIGHEST).reshape(
            (count_rows,) + shape_tail
        )
        return inner + jnp.einsum(
            "mk,mkij->mij", edge_weights, edges[:, :, part_index], precision=HIGHEST
        )

    return mix_terms(
        up_sum[:, 0],
        up_sum[:, 1],
        weighted(local_real, weight_real[:, :3], 0),
        weighted(local_real, weight_real[:, :3], 1),
        weighted(local_imag, weight_imag[:, :3], 0),
        weighted(local_imag, weight_imag[:, :3], 1),
    )


def body(
    tier_four,
    tier_six,
    tier_seven,
    coupling,
    eigenbasis,
    energies,
    decay_rates,
    bath_coefficients,
    occupation_five,
    local_five,
    peers_five,
    places_five,
    occupation_six,
    local_six,
    peers_six,
    places_six,
):
    count_rows = tier_four.shape[0]
    peer_count = lax.axis_size("mb")
    capacity = max(2, (12 * count_rows + 2 * peer_count - 1) // (2 * peer_count))
    matrix_shape = tier_four.shape[1:]
    column_ids = jnp.arange(4, dtype=jnp.int32)[None, :]
    wanted_five = (places_five + (column_ids >= 2).astype(jnp.int32) * count_rows).reshape(-1)
    raised_five, lowered_five = first_mode(tier_four, tier_six)
    table_five, placed_five = request_table(
        peers_five.reshape(-1), wanted_five, capacity, peer_count
    )
    got_five = fetch_plain(table_five, jnp.concatenate((tier_six, tier_four)))
    remote_five = pick_rows(got_five, placed_five).reshape((count_rows, 4) + matrix_shape)
    pair_real, pair_imag, other_real, other_imag = combine(
        tier_four,
        tier_six,
        raised_five,
        lowered_five,
        remote_five,
        local_five,
        occupation_five,
        bath_coefficients,
    )
    updated_five = settle(
        pair_real,
        pair_imag,
        other_real,
        other_imag,
        occupation_five,
        coupling,
        eigenbasis,
        energies,
        decay_rates,
    )
    raised_six, lowered_six = first_mode(updated_five, tier_seven)
    wanted_six = (places_six + (column_ids >= 2).astype(jnp.int32) * count_rows).reshape(-1)
    table_six, placed_six = request_table(peers_six.reshape(-1), wanted_six, capacity, peer_count)
    got_six = fetch_plain(table_six, jnp.concatenate((tier_seven, updated_five)))
    remote_six = pick_rows(got_six, placed_six).reshape((count_rows, 4) + matrix_shape)
    pair_real, pair_imag, other_real, other_imag = combine(
        updated_five,
        tier_seven,
        raised_six,
        lowered_six,
        remote_six,
        local_six,
        occupation_six,
        bath_coefficients,
    )
    updated_six = settle(
        pair_real,
        pair_imag,
        other_real,
        other_imag,
        occupation_six,
        coupling,
        eigenbasis,
        energies,
        decay_rates,
    )
    return (updated_five, updated_six)


def solution(mesh):
    in_specs = (
        P(("ma", "mb"), None, None, None),
        P(("ma", "mb"), None, None, None),
        P(("ma", "mb"), None, None, None),
        P(),
        P(),
        P(),
        P(),
        P(),
        P(("ma", "mb"), None),
        P(("ma", "mb"), None, None),
        P(("ma", "mb"), None),
        P(("ma", "mb"), None),
        P(("ma", "mb"), None),
        P(("ma", "mb"), None, None),
        P(("ma", "mb"), None),
        P(("ma", "mb"), None),
    )
    out_specs = (P(("ma", "mb"), None, None, None), P(("ma", "mb"), None, None, None))
    return jax.shard_map(body, mesh=mesh, in_specs=in_specs, out_specs=out_specs, check_vma=False)
```

profile of v0, /device:TPU:48, one launch (start us, length us, event | category | flops | bytes accessed | tf_op | source)
XLA Modules:
  0.0 393.5 jit_solution(6764957184308233637)
XLA Ops:
  0.6 0.8 copy.116
  2.7 0.8 broadcast_add_fusion
  4.3 0.7 all_to_all.22
  5.0 8.0 %all-to-all-start = ((s32[32,1,2]{2,1,0:T(1,128)}), s32[32,1,2]{2,1,0:T(1,128)S(1)}, u32[]{:S(2)}, u32[]{:S(2)}) async-start(s32[32,1,2]{2,1,0:T(1,128)} %bitcast.7), calls=%async_computation | async-start | bytes 32768 | tf_op jit(solution)/shard_map/all_to_all | solution.py:77
  13.1 0.8 copy.140
  15.1 1.7 pad_maximum_fusion
  18.3 0.8 all-to-all-done
  19.2 6.6 %all-to-all-start.2 = ((s32[32,1,2]{2,1,0:T(1,128)}), s32[32,1,2]{2,1,0:T(1,128)S(1)}, u32[]{:S(2)}, u32[]{:S(2)}) async-start(s32[32,1,2]{2,1,0:T(1,128)} %bitcast.67), calls=%async_computation.2 | async-start | bytes 32768 | tf_op jit(solution)/shard_map/all_to_all | solution.py:77
  26.0 4.3 %gather_fusion = f32[64,2,128,128]{3,2,1,0:T(8,128)} fusion(f32[16,2,128,128]{3,2,1,0:T(8,128)S(1)} %pad_maximum_fusion, s32[1024]{0:T(1024)S(1)} %pad_clamp_fusion.3), kind=kCustom, calls=%fused_computation | custom fusion | bytes 16777472 | tf_op jit(solution)/shard_map/gather | solution.py:77
  30.3 1.5 all-to-all-done.2
  31.8 6.1 %all-to-all-start.1 = ((f32[32,2,2,128,128]{4,3,2,1,0:T(8,128)}), f32[32,2,2,128,128]{4,3,2,1,0:T(8,128)}, u32[]{:S(2)}, u32[]{:S(2)}) async-start(f32[32,2,2,128,128]{4,3,2,1,0:T(8,128)} %bitcast.407), calls=%async_computation.1 | async-start | bytes 16777216 | tf_op jit(solution)/shard_map/all_to_all | solution.py:76
  38.1 1.4 collective-permute-start.1
  39.4 1.6 copy.114
  41.0 0.9 collective-permute-start
  43.9 119.1 %all-to-all-done.1 = f32[32,2,2,128,128]{4,3,2,1,0:T(8,128)} async-done(((f32[32,2,2,128,128]{4,3,2,1,0:T(8,128)}), f32[32,2,2,128,128]{4,3,2,1,0:T(8,128)}, u32[]{:S(2)}, u32[]{:S(2)}) %all-to-all-start.1) | async-done | bytes 8388640 | tf_op jit(solution)/shard_map/all_to_all | solution.py:76
  163.0 6.2 %gather_fusion.1 = f32[32,2,128,128]{3,2,1,0:T(8,128)} fusion(f32[64,2,128,128]{3,2,1,0:T(8,128)} %bitcast.10, s32[1024]{0:T(1024)S(1)} %pad_clamp_fusion.2), kind=kCustom, calls=%fused_computation.1 | custom fusion | bytes 8388736 | tf_op jit(solution)/shard_map/gather | solution.py:87
  169.2 1.8 slice.147
  171.0 1.6 fusion.19
  172.6 4.3 %fusion.10 = f32[8,1,128,128]{3,1,2,0:T(1,128)S(1)} fusion(f32[8,3,1,1]{1,2,3,0:T(1,128)S(1)} %bitcast.431, f32[8,3,128,128]{3,2,1,0:T(8,128)S(1)} %get-tuple-element.17), kind=kOutput, calls=%fused_computation.20 | convolution fusion | flops 4718592 | bytes 2097248 | tf_op jit(solution)/shard_map/mk,mkij->mij/dot_general | solution.py:120
  176.8 4.3 %fusion.12 = f32[8,1,128,128]{3,1,2,0:T(1,128)S(1)} fusion(f32[8,3,1,1]{1,2,3,0:T(1,128)S(1)} %bitcast.432, f32[8,3,128,128]{3,2,1,0:T(8,128)S(1)} %get-tuple-element.16), kind=kOutput, calls=%fused_computation.22 | convolution fusion | flops 4718592 | bytes 2097248 | tf_op jit(solution)/shard_map/mk,mkij->mij/dot_general | solution.py:120
  181.1 1.0 bitcast_add_fusion.2
  182.2 4.3 %fusion.14 = f32[8,1,128,128]{3,1,2,0:T(1,128)S(1)} fusion(f32[8,3,1,1]{1,2,3,0:T(1,128)S(1)} %bitcast.429, f32[8,3,128,128]{3,2,1,0:T(8,128)S(1)} %get-tuple-element.16), kind=kOutput, calls=%fused_computation.24 | convolution fusion | flops 4718592 | bytes 2097248 | tf_op jit(solution)/shard_map/mk,mkij->mij/dot_general | solution.py:120
  186.5 4.7 %fusion.8 = f32[8,1,128,128]{3,1,2,0:T(1,128)S(1)} fusion(f32[8,3,1,1]{1,2,3,0:T(1,128)S(1)} %bitcast.430, f32[8,3,128,128]{3,2,1,0:T(8,128)S(1)} %get-tuple-element.17), kind=kOutput, calls=%fused_computation.18 | convolution fusion | flops 4718592 | bytes 2097248 | tf_op jit(solution)/shard_map/mk,mkij->mij/dot_general | solution.py:120
  191.4 3.4 fusion.25
  194.7 1.1 fusion.145
  196.5 1.0 fusion.27
  198.1 1.0 fusion.107
  199.1 1.0 bitcast_add_fusion
  200.1 1.1 fusion.146
  201.9 1.0 fusion.28
  203.5 1.2 fusion.104
  204.7 1.1 convolution_bitcast_fusion.9
  205.8 1.1 convolution_bitcast_fusion.8
  206.9 1.0 fusion.101
  207.9 1.0 fusion.98
  209.1 4.3 %gather_fusion.2 = f32[64,2,128,128]{3,2,1,0:T(8,128)} fusion(f32[16,2,128,128]{3,2,0,1:T(8,128)S(1)} %maximum_maximum_fusion, s32[1024]{0:T(1024)S(1)} %pad_clamp_fusion.1), kind=kCustom, calls=%fused_computation.2 | custom fusion | bytes 16777472 | tf_op jit(solution)/shard_map/gather | solution.py:77
  213.4 7.1 %all-to-all-start.3 = ((f32[32,2,2,128,128]{4,3,2,1,0:T(8,128)}), f32[32,2,2,128,128]{4,3,2,1,0:T(8,128)}, u32[]{:S(2)}, u32[]{:S(2)}) async-start(f32[32,2,2,128,128]{4,3,2,1,0:T(8,128)} %bitcast.408), calls=%async_computation.3 | async-start | bytes 16777216 | tf_op jit(solution)/shard_map/all_to_all | solution.py:76
  220.5 1.6 copy.137
  222.7 1.6 collective-permute-start.3
  224.4 1.6 copy.325
  226.7 1.1 copy.161
  227.8 116.9 %all-to-all-done.3 = f32[32,2,2,128,128]{4,3,2,1,0:T(8,128)} async-done(((f32[32,2,2,128,128]{4,3,2,1,0:T(8,128)}), f32[32,2,2,128,128]{4,3,2,1,0:T(8,128)}, u32[]{:S(2)}, u32[]{:S(2)}) %all-to-all-start.3) | async-done | bytes 8388640 | tf_op jit(solution)/shard_map/all_to_all | solution.py:76
  344.7 6.2 %gather_fusion.3 = f32[32,2,128,128]{3,2,1,0:T(8,128)} fusion(f32[64,2,128,128]{3,2,1,0:T(8,128)} %bitcast.70, s32[1024]{0:T(1024)S(1)} %pad_clamp_fusion), kind=kCustom, calls=%fused_computation.3 | custom fusion | bytes 8388736 | tf_op jit(solution)/shard_map/gather | solution.py:87
  350.9 1.8 slice.154
  352.7 1.5 fusion.17
  354.2 4.5 %fusion.2 = f32[8,1,128,128]{3,1,2,0:T(1,128)S(1)} fusion(f32[8,3,1,1]{1,2,3,0:T(1,128)S(1)} %bitcast.427, f32[8,3,128,128]{3,2,1,0:T(8,128)S(1)} %get-tuple-element.15), kind=kOutput, calls=%fused_computation.12 | convolution fusion | flops 4718592 | bytes 2097248 | tf_op jit(solution)/shard_map/mk,mkij->mij/dot_general | solution.py:120
  358.7 4.3 %fusion.4 = f32[8,1,128,128]{3,1,2,0:T(1,128)S(1)} fusion(f32[8,3,1,1]{1,2,3,0:T(1,128)S(1)} %bitcast.428, f32[8,3,128,128]{3,2,1,0:T(8,128)S(1)} %get-tuple-element.14), kind=kOutput, calls=%fused_computation.14 | convolution fusion | flops 4718592 | bytes 2097248 | tf_op jit(solution)/shard_map/mk,mkij->mij/dot_general | solution.py:120
  363.0 1.0 convolution_add_fusion.4
  364.1 4.3 %fusion.6 = f32[8,1,128,128]{3,1,2,0:T(1,128)S(1)} fusion(f32[8,3,1,1]{1,2,3,0:T(1,128)S(1)} %bitcast.425, f32[8,3,128,128]{3,2,1,0:T(8,128)S(1)} %get-tuple-element.14), kind=kOutput, calls=%fused_computation.16 | convolution fusion | flops 4718592 | bytes 2097248 | tf_op jit(solution)/shard_map/mk,mkij->mij/dot_general | solution.py:120
  368.4 4.5 %fusion = f32[8,1,128,128]{3,1,2,0:T(1,128)S(1)} fusion(f32[8,3,1,1]{1,2,3,0:T(1,128)S(1)} %bitcast.426, f32[8,3,128,128]{3,2,1,0:T(8,128)S(1)} %get-tuple-element.15), kind=kOutput, calls=%fused_computation.10 | convolution fusion | flops 4718592 | bytes 2097248 | tf_op jit(solution)/shard_map/mk,mkij->mij/dot_general | solution.py:120
  373.2 1.0 copy-done.8
  374.1 3.3 fusion.23
  377.5 1.1 fusion.143
  379.3 1.0 fusion.30
  380.9 1.0 fusion.95
  381.9 1.0 convolution_add_fusion.2
  382.9 1.1 fusion.144
  384.7 1.0 fusion.31
  386.3 1.3 fusion.92
  387.6 1.1 convolution_bitcast_fusion.3
  388.7 1.1 convolution_bitcast_fusion.1
  389.8 1.0 convolution_bitcast_fusion.2
  390.8 1.0 convolution_bitcast_fusion
  391.9 1.1 copy.162
  (104 shorter events, 14.1 us)
Async XLA Ops:
  0.6 196.9 %copy-start = (f32[128,128]{1,0:T(8,128)S(1)}, f32[128,128]{1,0:T(8,128)}, u32[]{:S(2)}) copy-start(f32[128,128]{1,0:T(8,128)} %param.20) | copy-start | bytes 196612
  5.0 14.1 %all-to-all-start = ((s32[32,1,2]{2,1,0:T(1,128)}), s32[32,1,2]{2,1,0:T(1,128)S(1)}, u32[]{:S(2)}, u32[]{:S(2)}) async-start(s32[32,1,2]{2,1,0:T(1,128)} %bitcast.7), calls=%async_computation | async-start | bytes 32768 | tf_op jit(solution)/shard_map/all_to_all | solution.py:77
  19.2 12.7 %all-to-all-start.2 = ((s32[32,1,2]{2,1,0:T(1,128)}), s32[32,1,2]{2,1,0:T(1,128)S(1)}, u32[]{:S(2)}, u32[]{:S(2)}) async-start(s32[32,1,2]{2,1,0:T(1,128)} %bitcast.67), calls=%async_computation.2 | async-start | bytes 32768 | tf_op jit(solution)/shard_map/all_to_all | solution.py:77
  31.8 6.2 %copy-start.7 = (f32[8,2,128,128]{3,2,1,0:T(8,128)S(1)}, f32[8,2,128,128]{3,2,1,0:T(8,128)}, u32[]{:S(2)}) copy-start(f32[8,2,128,128]{3,2,1,0:T(8,128)} %param.16) | copy-start | bytes 3145732
  31.8 7.6 %copy-start.3 = (f32[8,2,128,128]{3,2,1,0:T(8,128)S(1)}, f32[8,2,128,128]{3,2,1,0:T(8,128)}, u32[]{:S(2)}) copy-start(f32[8,2,128,128]{3,2,1,0:T(8,128)} %param.17) | copy-start | bytes 3145732
  31.8 131.2 %all-to-all-start.1 = ((f32[32,2,2,128,128]{4,3,2,1,0:T(8,128)}), f32[32,2,2,128,128]{4,3,2,1,0:T(8,128)}, u32[]{:S(2)}, u32[]{:S(2)}) async-start(f32[32,2,2,128,128]{4,3,2,1,0:T(8,128)} %bitcast.407), calls=%async_computation.1 | async-start | bytes 16777216 | tf_op jit(solution)/shard_map/all_to_all | solution.py:76
  38.0 3.9 %copy-start.15 = (f32[2,12]{1,0:T(2,128)S(1)}, f32[2,12]{1,0:T(2,128)}, u32[]{:S(2)}) copy-start(f32[2,12]{1,0:T(2,128)} %param.23) | copy-start | bytes 292
  38.0 3.9 %copy-start.9 = (s32[8,12]{1,0:T(8,128)S(1)}, s32[8,12]{1,0:T(8,128)}, u32[]{:S(2)}) copy-start(s32[8,12]{1,0:T(8,128)} %param.24) | copy-start | bytes 1156
  38.0 3.9 copy-start.10
  38.0 4.7 %copy-start.11 = (s32[8,2,9]{2,1,0:T(2,128)S(1)}, s32[8,2,9]{2,1,0:T(2,128)}, u32[]{:S(2)}) copy-start(s32[8,2,9]{2,1,0:T(2,128)} %param.25) | copy-start | bytes 1732
  38.0 5.2 %copy-start.14 = (f32[12]{0:T(128)S(1)}, f32[12]{0:T(128)}, u32[]{:S(2)}) copy-start(f32[12]{0:T(128)} %param.22) | copy-start | bytes 148
  38.0 5.4 %copy-start.13 = (f32[128]{0:T(128)S(1)}, f32[128]{0:T(128)}, u32[]{:S(2)}) copy-start(f32[128]{0:T(128)} %param.21) | copy-start | bytes 1540
  38.1 132.9 %collective-permute-start.1 = (f32[8,2,128,128]{3,2,1,0:T(8,128)S(1)}, f32[8,2,128,128]{3,2,1,0:T(8,128)}, u32[]{:S(2)}, u32[]{:S(2)}) collective-permute-start(f32[8,2,128,128]{3,2,1,0:T(8,128)S(1)} %copy-done.7), channel_id=1, source_target_pairs={{0,32},{32,64},{64,96},{96,0},{1,33},{33,65},{65,97},{97,1},{2,34}... | collective-permute-start | bytes 3145736 | tf_op jit(solution)/shard_map/ppermute | solution.py:11
  41.0 150.4 %collective-permute-start = (f32[8,2,128,128]{3,0,2,1:T(8,128)}, f32[8,2,128,128]{3,0,2,1:T(8,128)}, u32[]{:S(2)}, u32[]{:S(2)}) collective-permute-start(f32[8,2,128,128]{3,0,2,1:T(8,128)} %copy.114), channel_id=1, source_target_pairs={{0,96},{32,0},{64,32},{96,64},{1,97},{33,1},{65,33},{97,65},{2,98}... | collective-permute-start | bytes 3145736 | tf_op jit(solution)/shard_map/ppermute | solution.py:11
  182.2 9.0 %copy-start.2 = (f32[32,2,128,128]{3,2,1,0:T(8,128)S(1)}, f32[32,2,128,128]{3,2,1,0:T(8,128)}, u32[]{:S(2)}) copy-start(f32[32,2,128,128]{3,2,1,0:T(8,128)} %gather_fusion.1) | copy-start | bytes 12582916
  194.7 1.1 copy-start.6
  206.9 2.0 copy-start.4
  213.4 7.1 %copy-start.5 = (f32[8,2,128,128]{3,2,1,0:T(8,128)S(1)}, f32[8,2,128,128]{3,2,1,0:T(8,128)}, u32[]{:S(2)}) copy-start(f32[8,2,128,128]{3,2,1,0:T(8,128)} %param.18) | copy-start | bytes 3145732
  213.4 131.2 %all-to-all-start.3 = ((f32[32,2,2,128,128]{4,3,2,1,0:T(8,128)}), f32[32,2,2,128,128]{4,3,2,1,0:T(8,128)}, u32[]{:S(2)}, u32[]{:S(2)}) async-start(f32[32,2,2,128,128]{4,3,2,1,0:T(8,128)} %bitcast.408), calls=%async_computation.3 | async-start | bytes 16777216 | tf_op jit(solution)/shard_map/all_to_all | solution.py:76
  222.1 3.9 copy-start.12
  222.1 151.0 %collective-permute-start.2 = (f32[8,2,128,128]{3,0,2,1:T(8,128)}, f32[8,2,128,128]{3,0,2,1:T(8,128)}, u32[]{:S(2)}, u32[]{:S(2)}) collective-permute-start(f32[8,2,128,128]{3,0,2,1:T(8,128)} %copy.137), channel_id=1, source_target_pairs={{0,96},{32,0},{64,32},{96,64},{1,97},{33,1},{65,33},{97,65},{2,98}... | collective-permute-start | bytes 3145736 | tf_op jit(solution)/shard_map/ppermute | solution.py:11
  222.7 130.0 %collective-permute-start.3 = (f32[8,2,128,128]{3,2,0,1:T(8,128)S(1)}, f32[8,2,128,128]{3,2,0,1:T(8,128)}, u32[]{:S(2)}, u32[]{:S(2)}) collective-permute-start(f32[8,2,128,128]{3,2,0,1:T(8,128)S(1)} %pad_maximum_fusion.3), channel_id=1, source_target_pairs={{0,32},{32,64},{64,96},{96,0},{1,33},{33,65},{65,97},{97,1},{2,34}... | collective-permute-start | bytes 3145736 | tf_op jit(solution)/shard_map/ppermute | solution.py:11
  364.1 8.8 %copy-start.1 = (f32[32,2,128,128]{3,2,1,0:T(8,128)S(1)}, f32[32,2,128,128]{3,2,1,0:T(8,128)}, u32[]{:S(2)}) copy-start(f32[32,2,128,128]{3,2,1,0:T(8,128)} %gather_fusion.3) | copy-start | bytes 12582916
  372.9 1.2 copy-start.8
where the time goes:
time: 398 us; the launch traced here: 393 us
  waiting for transfers between devices  238 us (60%)
  matrix products  73.3 us (18%)
  local copies, waits for them, and re-layouts  39.6 us (10%)
  starting transfers between devices  32.2 us (8%)
  other arithmetic  8.23 us (2%)
    all_to_all x2, waiting for transfers between devices, fetch_plain(): lax.all_to_all(store[lax.all_to_all(table, 'mb', split_axis=0, concat_axi...  236 us
    dot_general x8, matrix products, weighted(): jnp.einsum('mk,mkij->mij', edge_weights, edges[:, :, part_index], precisi...  35.1 us
    all_to_all x2, starting transfers between devices, fetch_plain(): lax.all_to_all(table, 'mb', split_axis=0, concat_axis=0, tiled=True)  14.6 us
    all_to_all x2, starting transfers between devices, fetch_plain(): lax.all_to_all(store[lax.all_to_all(table, 'mb', split_axis=0, concat_axi...  13.2 us
    gather x2, local copies, waits for them, and re-layouts, pick_rows(): return flat_rows[placed]  12.3 us
    dot_general x12, matrix products, right_product(): return jnp.einsum('mij,jk->mik', batch, matrix, precision=HIGHEST)  11.1 us
    dot_general x12, matrix products, left_product(): return jnp.einsum('ij,mjk->mik', matrix, batch, precision=HIGHEST)  10.7 us
    unnamed x41, local copies, waits for them, and re-layouts  10.2 us
  transfers between devices with their start and end apart: 8, of which 4 were waited for; matrix products, arithmetic and copies ran while one was open for 19% of the time, Pallas kernels for 0%

commit v1 on v0

v1 whole, which is shorter than its diff:
```python
import functools

import jax
import jax.numpy as jnp
from jax import lax
from jax.experimental import pallas as pl
from jax.experimental.pallas import tpu as pltpu
from jax.sharding import PartitionSpec as P

MESH = pl.DeviceIdType.MESH
F32, BF16 = jnp.float32, jnp.bfloat16
PARTS = 4
STRIDE = 11
LOWER_AT, COUNT_AT, TIER_AT = 11, 22, 64


def halves(x):
    high = x.astype(BF16)
    return high, (x - high.astype(F32)).astype(BF16)


def mxu(a, b):
    return jnp.dot(a, b, preferred_element_type=F32)


def dot3(a, b):
    return mxu(a[0], b[0]) + (mxu(a[0], b[1]) + mxu(a[1], b[0]))


def sweep_kernel(
    peers,
    rows,
    block,
    x4,
    x6,
    x7,
    tab_in,
    coupling,
    basis,
    energies,
    occ5,
    occ6,
    decay,
    bath,
    out5_hbm,
    out6_hbm,
    tab,
    s64,
    s7,
    s5,
    sums5,
    sums6,
    got5,
    got6,
    raised5,
    lowered5,
    raised6,
    lowered6,
    out5,
    out6,
    weights,
    stack,
    wide,
    left,
    split_sq,
    send_sems,
    recv_sems,
    own_sems,
    home_recv,
    home_own,
    out_sems,
):
    total = peers * block
    part = block // PARTS
    ma, me = lax.axis_index("ma"), lax.axis_index("mb")
    above = lax.rem(ma + 1, rows)
    below = lax.rem(ma + rows - 1, rows)

    def peer_of(j):
        return lax.rem(me + lax.rem(j * STRIDE, peers), peers)

    def each_peer(fn):
        def step(j, carry):
            fn(peer_of(j))
            return carry

        lax.fori_loop(1, peers, step, 0)

    def tile(d):
        return pl.ds(pl.multiple_of(d * 8, 8), 8)

    def remote(src, dst, k, recv, device):
        return pltpu.make_async_remote_copy(
            src_ref=src,
            dst_ref=dst,
            send_sem=send_sems.at[k],
            recv_sem=recv,
            device_id=device,
            device_id_type=MESH,
        )

    def arrived(ref, recv):
        remote(ref, ref, 0, recv, (ma, peer_of(1))).wait_recv()

    def sent(ref, k):
        remote(ref, ref, k, recv_sems.at[0], (ma, peer_of(1))).wait_send()

    barrier = pltpu.get_barrier_semaphore()
    each_peer(lambda d: pl.semaphore_signal(barrier, inc=1, device_id=(ma, d), device_id_type=MESH))
    pl.semaphore_signal(barrier, inc=1, device_id=(above, me), device_id_type=MESH)
    pl.semaphore_signal(barrier, inc=1, device_id=(below, me), device_id_type=MESH)

    mine = pl.ds(pl.multiple_of(me * block, block), block)
    own = [
        pltpu.make_async_copy(tab_in, tab.at[mine], own_sems.at[0]),
        pltpu.make_async_copy(x6.at[:, tile(me), :], s64.at[0, mine], own_sems.at[1]),
        pltpu.make_async_copy(x4.at[:, tile(me), :], s64.at[1, mine], own_sems.at[2]),
        pltpu.make_async_copy(x7.at[:, tile(me), :], s7.at[mine], own_sems.at[3]),
    ]
    for copy in own:
        copy.start()
    pl.semaphore_wait(barrier, peers + 1)

    def send_tables(d):
        remote(tab_in, tab.at[mine], 0, recv_sems.at[0], (ma, d)).start()

    def send_first(d):
        remote(x6.at[:, tile(d), :], s64.at[0, mine], 1, recv_sems.at[1], (ma, d)).start()
        remote(x4.at[:, tile(d), :], s64.at[1, mine], 1, recv_sems.at[1], (ma, d)).start()

    def send_seven(half):
        some = pl.ds(half * (block // 2), block // 2)
        there = pl.ds(pl.multiple_of(me * block + half * (block // 2), block // 2), block // 2)

        def fn(d):
            remote(x7.at[some, tile(d), :], s7.at[there], 2, recv_sems.at[2], (ma, d)).start()

        each_peer(fn)

    each_peer(send_tables)
    each_peer(send_first)
    ring = [
        remote(x6, raised5, 3, recv_sems.at[3], (below, me)),
        remote(x4, lowered5, 4, recv_sems.at[4], (above, me)),
        remote(x7, raised6, 5, recv_sems.at[5], (below, me)),
    ]
    for copy in ring:
        copy.start()
    send_seven(0)

    e = basis[...]
    c = coupling[...]
    turned = jnp.transpose(e)
    e2, c2, t2 = halves(e), halves(c), halves(turned)
    wide[0], wide[1] = e2
    wide[2], wide[3] = t2
    wide[4], wide[5] = halves(dot3(c2, e2))
    left[0, :, 0:128], left[1, :, 0:128] = halves(dot3(t2, c2))
    minus = halves(-turned)
    left[0, :, 128:256], left[1, :, 128:256] = minus
    across = jnp.broadcast_to(energies[...], (128, 128))
    split = jnp.transpose(across) - across
    split_sq[0] = split
    split_sq[1] = split * split

    own[0].wait()
    arrived(tab.at[pl.ds(0, total - block)], recv_sems.at[0])
    WR = 32

    def weigh(tier):
        def step(i, carry):
            at = pl.ds(pl.multiple_of(i * WR, WR), WR)
            t = tab[at, :]
            column = lax.broadcasted_iota(jnp.int32, (WR, total), 1)
            up = jnp.zeros((WR, total), F32)
            real = jnp.zeros((WR, total), F32)
            imag = jnp.zeros((WR, total), F32)
            for k in range(LOWER_AT):
                base = tier * TIER_AT + k
                hit = t[:, base : base + 1] == column
                up = up + jnp.where(hit, 1.0, 0.0)
                hit = t[:, base + LOWER_AT : base + LOWER_AT + 1] == column
                n = t[:, base + COUNT_AT : base + COUNT_AT + 1].astype(F32)
                real = real + jnp.where(hit, n * bath[0, k + 1], 0.0)
                imag = imag + jnp.where(hit, n * bath[1, k + 1], 0.0)
            rh, rl = halves(real)
            ih, il = halves(imag)
            u = up.astype(BF16)
            for spot, value in enumerate((u, u, rh, rh, rl)):
                weights[tier, 0, at, spot * total : (spot + 1) * total] = value
            for spot, value in enumerate((ih, ih, il)):
                weights[tier, 1, at, (spot + 2) * total : (spot + 3) * total] = value
            return carry

        lax.fori_loop(0, total // WR, step, 0)

    weigh(0)
    weigh(1)

    def prepare(flat, spots_high, spot_low):
        for s in range(8):
            high, low = halves(flat[pl.ds(s, total, stride=8), :])
            lanes = slice(128 * s, 128 * s + 128)
            for spot in spots_high:
                stack[spot * total : (spot + 1) * total, lanes] = high
            stack[spot_low * total : (spot_low + 1) * total, lanes] = low

    def combine(tier, sums):
        flat = sums.reshape(total * 16, 128)
        for pair in range(4):
            lanes = slice(256 * pair, 256 * pair + 256)
            a = mxu(weights[tier, 0], stack[:, lanes])
            b = mxu(weights[tier, 1, :, 2 * total :], stack[2 * total :, lanes])
            for t in range(2):
                s = 2 * pair + t
                flat[pl.ds(s, total, stride=16), :] = a[:, 128 * t : 128 * t + 128]
                flat[pl.ds(8 + s, total, stride=16), :] = b[:, 128 * t : 128 * t + 128]

    def send_home(tier, sums, got):
        def step(q, carry):
            here = pl.ds(q * part, part)
            at = pl.multiple_of(me * block + q * part, part)
            pltpu.make_async_copy(
                sums.at[pl.ds(at, part)], got.at[here, :, tile(me), :], home_own.at[tier, q]
            ).start()

            def fn(d):
                start = pl.multiple_of(d * block + q * part, part)
                remote(
                    sums.at[pl.ds(start, part)],
                    got.at[here, :, tile(me), :],
                    6 + tier,
                    home_recv.at[tier, q],
                    (ma, d),
                ).start()

            each_peer(fn)
            return carry

        lax.fori_loop(0, PARTS, step, 0)

    def got_home(tier, sums, got, q):
        here = pl.ds(q * part, part)
        at = pl.multiple_of(me * block + q * part, part)
        pltpu.make_async_copy(
            sums.at[pl.ds(at, part)], got.at[here, :, tile(me), :], home_own.at[tier, q]
        ).wait()
        arrived(got.at[here, :, pl.ds(0, 8 * (peers - 1)), :], home_recv.at[tier, q])

    def right(x, spot):
        return dot3(halves(x), (wide[spot], wide[spot + 1]))

    def settle(m, got, raised, lowered, occ, out):
        n = occ[m, 0].astype(F32)
        low = lowered[m]
        a = got[m, 0] + raised[m] + (n * bath[0, 0]) * low
        b = got[m, 1] + (n * bath[1, 0]) * low
        ar, ai, br, bi = a[0:128], a[128:256], b[0:128], b[128:256]
        first = right(jnp.concatenate([ar - bi, ai + br], axis=0), 0)
        second = right(jnp.concatenate([ar + bi, ai - br], axis=0), 4)
        both = jnp.concatenate(
            [
                jnp.concatenate([first[0:128], first[128:256]], axis=1),
                jnp.concatenate([second[0:128], second[128:256]], axis=1),
            ],
            axis=0,
        )
        comm = dot3((left[0], left[1]), halves(both))
        eigen_real, eigen_imag = -comm[:, 128:256], comm[:, 0:128]
        damping = jnp.float32(0.0)
        for k in range(12):
            damping = damping + occ[m, k].astype(F32) * decay[k]
        inverse = 1.0 / (damping * damping + split_sq[1])
        factor_real = -damping * inverse
        factor_imag = split_sq[0] * inverse
        solved = jnp.concatenate(
            [
                eigen_real * factor_real - eigen_imag * factor_imag,
                eigen_real * factor_imag + eigen_imag * factor_real,
            ],
            axis=0,
        )
        half = right(solved, 2)
        back = dot3(
            (wide[0], wide[1]),
            halves(jnp.concatenate([half[0:128], half[128:256]], axis=1)),
        )
        out[m, 0:128, :] = back[:, 0:128]
        out[m, 128:256, :] = back[:, 128:256]

    own[1].wait()
    own[2].wait()
    arrived(s64.at[:, pl.ds(0, total - block)], recv_sems.at[1])
    prepare(s64.at[0].reshape(total * 8, 128), (0,), 1)
    prepare(s64.at[1].reshape(total * 8, 128), (2, 4), 3)
    combine(0, sums5)
    send_home(0, sums5, got5)
    send_seven(1)
    arrived(raised5, recv_sems.at[3])
    arrived(lowered5, recv_sems.at[4])

    def tier_five(q, carry):
        got_home(0, sums5, got5, q)
        for r in range(part):
            settle(q * part + r, got5, raised5, lowered5, occ5, out5)
        here = pl.ds(q * part, part)
        there = pl.ds(pl.multiple_of(me * block + q * part, part), part)

        def fn(d):
            remote(out5.at[here, tile(d), :], s5.at[there], 8, recv_sems.at[6], (ma, d)).start()

        each_peer(fn)
        remote(out5.at[here], lowered6.at[here], 9, recv_sems.at[7], (above, me)).start()
        pltpu.make_async_copy(out5.at[here, tile(me), :], s5.at[there], own_sems.at[4]).start()
        pltpu.make_async_copy(out5.at[here], out5_hbm.at[here], out_sems.at[0]).start()
        return carry

    lax.fori_loop(0, PARTS, tier_five, 0)

    own[3].wait()
    arrived(s7.at[pl.ds(0, total - block)], recv_sems.at[2])
    prepare(s7.reshape(total * 8, 128), (0,), 1)
    pltpu.make_async_copy(s5.at[mine], s5.at[mine], own_sems.at[4]).wait()
    arrived(s5.at[pl.ds(0, total - block)], recv_sems.at[6])
    prepare(s5.reshape(total * 8, 128), (2, 4), 3)
    combine(1, sums6)
    send_home(1, sums6, got6)
    arrived(raised6, recv_sems.at[5])
    arrived(lowered6, recv_sems.at[7])

    def tier_six(q, carry):
        got_home(1, sums6, got6, q)
        for r in range(part):
            settle(q * part + r, got6, raised6, lowered6, occ6, out6)
        here = pl.ds(q * part, part)
        pltpu.make_async_copy(out6.at[here], out6_hbm.at[here], out_sems.at[1]).start()
        return carry

    lax.fori_loop(0, PARTS, tier_six, 0)

    most = pl.ds(0, total - block)
    sent(tab.at[most], 0)
    sent(s64.at[:, most], 1)
    sent(s7.at[most], 2)
    for k, copy in enumerate(ring):
        copy.wait_send()
    sent(sums5.at[most], 6)
    sent(sums6.at[most], 7)
    sent(s5.at[most], 8)
    sent(lowered6, 9)
    pltpu.make_async_copy(out5, out5_hbm, out_sems.at[0]).wait()
    pltpu.make_async_copy(out6, out6_hbm, out_sems.at[1]).wait()


def table_of(local, peers, places, occupation, block):
    base = lax.axis_index("mb").astype(jnp.int32) * block
    remote = peers * block + places
    near = local + base
    return jnp.concatenate(
        [remote[:, :2], near[:, 0], remote[:, 2:], near[:, 1], occupation[:, 1:]], axis=1
    )


def body(
    rows,
    peers,
    tier_four,
    tier_six,
    tier_seven,
    coupling,
    eigenbasis,
    energies,
    decay_rates,
    bath_coefficients,
    occupation_five,
    local_five,
    peers_five,
    places_five,
    occupation_six,
    local_six,
    peers_six,
    places_six,
):
    block = tier_four.shape[0]
    total = peers * block
    shape = tier_four.shape
    table = jnp.concatenate(
        [
            jnp.pad(table_of(local_five, peers_five, places_five, occupation_five, block), ((0, 0), (0, 31))),
            jnp.pad(table_of(local_six, peers_six, places_six, occupation_six, block), ((0, 0), (0, 31))),
        ],
        axis=1,
    )
    flat = (block, 256, 128)
    any_space = pl.BlockSpec(memory_space=pl.ANY)
    vmem = pl.BlockSpec(memory_space=pltpu.VMEM)
    smem = pl.BlockSpec(memory_space=pltpu.SMEM)
    out = jax.ShapeDtypeStruct(flat, F32)
    store = pltpu.VMEM((total, 8, 128), F32)
    sums = pltpu.VMEM((total, 2, 8, 128), F32)
    got = pltpu.VMEM((block, 2, 256, 128), F32)
    whole = pltpu.VMEM(flat, F32)
    dma = pltpu.SemaphoreType.DMA
    five, six = pl.pallas_call(
        functools.partial(sweep_kernel, peers, rows, block),
        out_shape=(out, out),
        in_specs=[any_space] * 3 + [vmem] * 4 + [smem] * 4,
        out_specs=(any_space, any_space),
        scratch_shapes=[
            pltpu.VMEM((total, 128), jnp.int32),
            pltpu.VMEM((2, total, 8, 128), F32),
            store,
            store,
            sums,
            sums,
            got,
            got,
            whole,
            whole,
            whole,
            whole,
            whole,
            whole,
            pltpu.VMEM((2, 2, total, 5 * total), BF16),
            pltpu.VMEM((5 * total, 1024), BF16),
            pltpu.VMEM((6, 128, 128), BF16),
            pltpu.VMEM((2, 128, 256), BF16),
            pltpu.VMEM((2, 128, 128), F32),
            dma((10,)),
            dma((8,)),
            dma((5,)),
            dma((2, PARTS)),
            dma((2, PARTS)),
            dma((2,)),
        ],
        compiler_params=pltpu.CompilerParams(
            collective_id=0, has_side_effects=True, vmem_limit_bytes=60 * 1024 * 1024
        ),
        name="sweep",
    )(
        tier_four.reshape(flat),
        tier_six.reshape(flat),
        tier_seven.reshape(flat),
        table,
        coupling,
        eigenbasis,
        energies.reshape(1, -1),
        occupation_five,
        occupation_six,
        decay_rates,
        bath_coefficients,
    )
    return five.reshape(shape), six.reshape(shape)


def solution(mesh):
    rows, peers = mesh.shape["ma"], mesh.shape["mb"]
    whole = P(("ma", "mb"), None, None, None)
    wide = P(("ma", "mb"), None)
    tables = (wide, P(("ma", "mb"), None, None), wide, wide)
    in_specs = (whole,) * 3 + (P(),) * 5 + tables + tables
    return jax.shard_map(
        functools.partial(body, rows, peers),
        mesh=mesh,
        in_specs=in_specs,
        out_specs=(whole, whole),
        check_vma=False,
    )
```

time: 398 us -> 123 us (0.31)
  the two profiles are of different devices: /device:TPU:48 before, /device:TPU:1 now
where the time goes in v1:
time: 123 us; the launch traced here: 122 us
  Pallas kernels  112 us (91%)
  local copies, waits for them, and re-layouts  8.62 us (7%)
    pallas_call x1, Pallas kernels, body(): pl.pallas_call(functools.partial(sweep_kernel, peers, rows, block), out_s...  112 us
    unnamed x24, local copies, waits for them, and re-layouts  8.16 us

profile of v1, /device:TPU:1, one launch (start us, length us, event | category | flops | bytes accessed | tf_op | source)
XLA Modules:
  0.0 122.3 jit_solution(5936671498804745753)
XLA Ops:
  0.6 0.0 copy-start.5
  0.6 0.7 copy-done.5
  1.3 0.0 copy-start.6
  1.3 0.1 copy.18
  1.4 0.6 copy-done.6
  2.0 0.1 copy.19
  2.1 0.0 copy-start.7
  2.1 0.7 copy-done.7
  2.8 0.0 copy-start.8
  2.8 0.1 copy.21
  2.8 0.6 copy-done.8
  3.4 0.1 copy.22
  3.5 0.0 copy-start.2
  3.5 0.7 copy-done.2
  4.2 0.0 copy-start.1
  4.2 0.1 slice.34
  4.3 0.6 copy-done.1
  4.9 0.1 slice.39
  5.0 0.1 fusion.1
  5.0 0.0 copy-start.3
  5.0 0.0 copy-start.4
  5.0 0.1 fusion
  5.1 0.6 copy-done.3
  5.7 0.0 copy-done.4
  5.8 0.1 concatenate.10
  5.9 0.1 concatenate.9
  5.9 0.7 pad_add_fusion.tab_in
  6.6 112.3 %sweep.1 = (f32[8,256,128]{2,1,0:T(8,128)}, f32[8,256,128]{2,1,0:T(8,128)}) custom-call(f32[8,256,128]{2,1,0:T(8,128)} %bitcast.14, f32[8,256,128]{2,1,0:T(8,128)} %bitcast.15, f32[8,256,128]{2,1,0:T(8,128)} %bitcast.16, s32[8,128]{1,0:T(8,128)} %pad_add_fusion.tab_in, f32[128,128]{1,0:T(8,128)} %coupling.1, f32[128,128]{1,0:T(8,128)} %basis.1, ...), custom_call_target="tpu_custom_call" | custom-call | tf_op jit(solution)/shard_map/sweep/pallas_call | solution.py:404
  119.0 0.0 copy-start
  119.0 2.4 %copy.28 = f32[8,2,128,128]{3,2,1,0:T(8,128)} copy(f32[8,2,128,128]{3,2,1,0:T(8,128)} %bitcast.18) | data formatting | bytes 2097152
  121.4 0.0 copy-done
  121.4 1.0 copy.29
  (5 shorter events, 0.0 us)
Async XLA Ops:
  0.6 0.7 copy-start.5
  1.3 0.7 copy-start.6
  2.1 0.7 copy-start.7
  2.8 0.7 copy-start.8
  3.5 0.7 copy-start.2
  4.2 0.7 copy-start.1
  5.0 0.7 copy-start.3
  5.0 0.7 copy-start.4
  119.0 2.4 %copy-start = (f32[8,256,128]{2,1,0:T(8,128)S(1)}, f32[8,256,128]{2,1,0:T(8,128)}, u32[]{:S(2)}) copy-start(f32[8,256,128]{2,1,0:T(8,128)} %get-tuple-element.5) | copy-start | bytes 3145732

commit v2 on v1

--- a/solution.py
+++ b/solution.py
@@ -11,7 +11,7 @@
 F32, BF16 = jnp.float32, jnp.bfloat16
 PARTS = 4
 STRIDE = 11
-LOWER_AT, COUNT_AT, TIER_AT = 11, 22, 64
+LOWER_AT, REAL_AT, IMAG_AT, TIER_AT = 11, 22, 33, 64
 
 
 def halves(x):
@@ -34,16 +34,26 @@
     x4,
     x6,
     x7,
+    *refs,
+):
+    small, refs = refs[:13], refs[13:]
+    out5, out6, *refs = refs
+    local, refs = refs[:13], refs[13:]
+    run(peers, rows, block, x4, x6, x7, small, local, out5, out6, *refs)
+
+
+def run(
+    peers,
+    rows,
+    block,
+    x4,
+    x6,
+    x7,
+    small,
+    local,
+    out5,
+    out6,
     tab_in,
-    coupling,
-    basis,
-    energies,
-    occ5,
-    occ6,
-    decay,
-    bath,
-    out5_hbm,
-    out6_hbm,
     tab,
     s64,
     s7,
@@ -56,19 +66,18 @@
     lowered5,
     raised6,
     lowered6,
-    out5,
-    out6,
     weights,
     stack,
     wide,
     left,
     split_sq,
+    rates,
     send_sems,
     recv_sems,
     own_sems,
     home_recv,
     home_own,
-    out_sems,
+    small_sems,
 ):
     total = peers * block
     part = block // PARTS
@@ -105,6 +114,13 @@
     def sent(ref, k):
         remote(ref, ref, k, recv_sems.at[0], (ma, peer_of(1))).wait_send()
 
+    fetch = [
+        pltpu.make_async_copy(a, b, small_sems.at[i]) for i, (a, b) in enumerate(zip(small, local))
+    ]
+    for copy in fetch:
+        copy.start()
+    coupling, basis, energies, decay, bath, *tables = local
+
     barrier = pltpu.get_barrier_semaphore()
     each_peer(lambda d: pl.semaphore_signal(barrier, inc=1, device_id=(ma, d), device_id_type=MESH))
     pl.semaphore_signal(barrier, inc=1, device_id=(above, me), device_id_type=MESH)
@@ -117,8 +133,43 @@
         pltpu.make_async_copy(x4.at[:, tile(me), :], s64.at[1, mine], own_sems.at[2]),
         pltpu.make_async_copy(x7.at[:, tile(me), :], s7.at[mine], own_sems.at[3]),
     ]
-    for copy in own:
+    for copy in own[1:]:
         copy.start()
+    for copy in fetch:
+        copy.wait()
+    lane = lax.broadcasted_iota(jnp.int32, (block, 128), 1)
+    on_diagonal = lax.broadcasted_iota(jnp.int32, (block, block), 0) == lax.broadcasted_iota(
+        jnp.int32, (block, block), 1
+    )
+    entries = jnp.zeros((block, 128), F32)
+
+    def put(entries, at, column):
+        return jnp.where(lane == at, jnp.broadcast_to(column, (block, 128)), entries)
+
+    for tier in range(2):
+        occupation, near, peer_ids, places = tables[4 * tier : 4 * tier + 4]
+        base = tier * TIER_AT
+        wanted = (peer_ids[...] * block + places[...]).astype(F32)
+        for k in range(4):
+            row = jnp.broadcast_to(wanted[k : k + 1, :], (block, block))
+            column = jnp.sum(jnp.where(on_diagonal, row, 0.0), axis=1, keepdims=True)
+            entries = put(entries, base + (k if k < 2 else LOWER_AT + k - 2), column)
+        inside = (near[...] + me * block).astype(F32)
+        up, low = inside[:, 0, :], inside[:, 1, :]
+        for k in range(9):
+            entries = put(entries, base + 2 + k, up[:, k : k + 1])
+            entries = put(entries, base + LOWER_AT + 2 + k, low[:, k : k + 1])
+        counted = occupation[...].astype(F32)
+        real = counted * bath[0:1, :]
+        imag = counted * bath[1:2, :]
+        for k in range(11):
+            entries = put(entries, base + REAL_AT + k, real[:, k + 1 : k + 2])
+            entries = put(entries, base + IMAG_AT + k, imag[:, k + 1 : k + 2])
+        damp = jnp.sum(counted * decay[...], axis=1, keepdims=True)
+        for spot, column in enumerate((real[:, 0:1], imag[:, 0:1], damp)):
+            rates[tier, spot] = jnp.broadcast_to(column, (block, 128))
+    tab_in[...] = entries
+    own[0].start()
     pl.semaphore_wait(barrier, peers + 1)
 
     def send_tables(d):
@@ -171,7 +222,7 @@
         def step(i, carry):
             at = pl.ds(pl.multiple_of(i * WR, WR), WR)
             t = tab[at, :]
-            column = lax.broadcasted_iota(jnp.int32, (WR, total), 1)
+            column = lax.broadcasted_iota(jnp.int32, (WR, total), 1).astype(F32)
             up = jnp.zeros((WR, total), F32)
             real = jnp.zeros((WR, total), F32)
             imag = jnp.zeros((WR, total), F32)
@@ -180,9 +231,8 @@
                 hit = t[:, base : base + 1] == column
                 up = up + jnp.where(hit, 1.0, 0.0)
                 hit = t[:, base + LOWER_AT : base + LOWER_AT + 1] == column
-                n = t[:, base + COUNT_AT : base + COUNT_AT + 1].astype(F32)
-                real = real + jnp.where(hit, n * bath[0, k + 1], 0.0)
-                imag = imag + jnp.where(hit, n * bath[1, k + 1], 0.0)
+                real = real + jnp.where(hit, t[:, base + REAL_AT : base + REAL_AT + 1], 0.0)
+                imag = imag + jnp.where(hit, t[:, base + IMAG_AT : base + IMAG_AT + 1], 0.0)
             rh, rl = halves(real)
             ih, il = halves(imag)
             u = up.astype(BF16)
@@ -205,56 +255,61 @@
                 stack[spot * total : (spot + 1) * total, lanes] = high
             stack[spot_low * total : (spot_low + 1) * total, lanes] = low
 
-    def combine(tier, sums):
-        flat = sums.reshape(total * 16, 128)
+    def combine(tier, kind, sums):
+        flat = sums.at[kind].reshape(total * 8, 128)
+        first = 2 * kind * total
         for pair in range(4):
             lanes = slice(256 * pair, 256 * pair + 256)
-            a = mxu(weights[tier, 0], stack[:, lanes])
-            b = mxu(weights[tier, 1, :, 2 * total :], stack[2 * total :, lanes])
+            a = mxu(weights[tier, kind, :, first:], stack[first:, lanes])
             for t in range(2):
-                s = 2 * pair + t
-                flat[pl.ds(s, total, stride=16), :] = a[:, 128 * t : 128 * t + 128]
-                flat[pl.ds(8 + s, total, stride=16), :] = b[:, 128 * t : 128 * t + 128]
-
-    def send_home(tier, sums, got):
+                flat[pl.ds(2 * pair + t, total, stride=8), :] = a[:, 128 * t : 128 * t + 128]
+
+    def send_home(tier, kind, sums, got, q, size):
+        here = pl.ds(pl.multiple_of(q * size, size), size)
+        slot = home_own.at[tier, q] if kind == 0 else home_own.at[tier, PARTS]
+        recv = home_recv.at[tier, q] if kind == 0 else home_recv.at[tier, PARTS]
+        at = pl.multiple_of(me * block + q * size, size)
+        pltpu.make_async_copy(
+            sums.at[kind, pl.ds(at, size)], got.at[kind, here, tile(me), :], slot
+        ).start()
+
+        def fn(d):
+            start = pl.multiple_of(d * block + q * size, size)
+            remote(
+                sums.at[kind, pl.ds(start, size)],
+                got.at[kind, here, tile(me), :],
+                6 + tier,
+                recv,
+                (ma, d),
+            ).start()
+
+        each_peer(fn)
+
+    def send_parts(tier, sums, got):
         def step(q, carry):
-            here = pl.ds(q * part, part)
-            at = pl.multiple_of(me * block + q * part, part)
-            pltpu.make_async_copy(
-                sums.at[pl.ds(at, part)], got.at[here, :, tile(me), :], home_own.at[tier, q]
-            ).start()
-
-            def fn(d):
-                start = pl.multiple_of(d * block + q * part, part)
-                remote(
-                    sums.at[pl.ds(start, part)],
-                    got.at[here, :, tile(me), :],
-                    6 + tier,
-                    home_recv.at[tier, q],
-                    (ma, d),
-                ).start()
-
-            each_peer(fn)
+            send_home(tier, 0, sums, got, q, part)
             return carry
 
         lax.fori_loop(0, PARTS, step, 0)
 
-    def got_home(tier, sums, got, q):
-        here = pl.ds(q * part, part)
-        at = pl.multiple_of(me * block + q * part, part)
-        pltpu.make_async_copy(
-            sums.at[pl.ds(at, part)], got.at[here, :, tile(me), :], home_own.at[tier, q]
-        ).wait()
-        arrived(got.at[here, :, pl.ds(0, 8 * (peers - 1)), :], home_recv.at[tier, q])
+    def got_home(tier, kind, got, q, size):
+        here = pl.ds(pl.multiple_of(q * size, size), size)
+        slot = home_own.at[tier, q] if kind == 0 else home_own.at[tier, PARTS]
+        recv = home_recv.at[tier, q] if kind == 0 else home_recv.at[tier, PARTS]
+        ref = got.at[kind, here, tile(me), :]
+        pltpu.make_async_copy(ref, ref, slot).wait()
+        arrived(got.at[kind, here, pl.ds(0, 8 * (peers - 1)), :], recv)
 
     def right(x, spot):
         return dot3(halves(x), (wide[spot], wide[spot + 1]))
 
-    def settle(m, got, raised, lowered, occ, out):
-        n = occ[m, 0].astype(F32)
+    def settle(tier, m, got, raised, lowered, out):
         low = lowered[m]
-        a = got[m, 0] + raised[m] + (n * bath[0, 0]) * low
-        b = got[m, 1] + (n * bath[1, 0]) * low
+        real = rates[tier, 0, pl.ds(m, 1), :]
+        imag = rates[tier, 1, pl.ds(m, 1), :]
+        damping = jnp.broadcast_to(rates[tier, 2, pl.ds(m, 1), :], (128, 128))
+        a = got[0, m] + raised[m] + real * low
+        b = got[1, m] + imag * low
         ar, ai, br, bi = a[0:128], a[128:256], b[0:128], b[128:256]
         first = right(jnp.concatenate([ar - bi, ai + br], axis=0), 0)
         second = right(jnp.concatenate([ar + bi, ai - br], axis=0), 4)
@@ -267,9 +322,6 @@
         )
         comm = dot3((left[0], left[1]), halves(both))
         eigen_real, eigen_imag = -comm[:, 128:256], comm[:, 0:128]
-        damping = jnp.float32(0.0)
-        for k in range(12):
-            damping = damping + occ[m, k].astype(F32) * decay[k]
         inverse = 1.0 / (damping * damping + split_sq[1])
         factor_real = -damping * inverse
         factor_imag = split_sq[0] * inverse
@@ -293,16 +345,18 @@
     arrived(s64.at[:, pl.ds(0, total - block)], recv_sems.at[1])
     prepare(s64.at[0].reshape(total * 8, 128), (0,), 1)
     prepare(s64.at[1].reshape(total * 8, 128), (2, 4), 3)
-    combine(0, sums5)
-    send_home(0, sums5, got5)
-    send_seven(1)
+    combine(0, 1, sums5)
+    send_home(0, 1, sums5, got5, 0, block)
+    combine(0, 0, sums5)
+    send_parts(0, sums5, got5)
     arrived(raised5, recv_sems.at[3])
     arrived(lowered5, recv_sems.at[4])
+    got_home(0, 1, got5, 0, block)
 
     def tier_five(q, carry):
-        got_home(0, sums5, got5, q)
+        got_home(0, 0, got5, q, part)
         for r in range(part):
-            settle(q * part + r, got5, raised5, lowered5, occ5, out5)
+            settle(0, q * part + r, got5, raised5, lowered5, out5)
         here = pl.ds(q * part, part)
         there = pl.ds(pl.multiple_of(me * block + q * part, part), part)
 
@@ -312,28 +366,29 @@
         each_peer(fn)
         remote(out5.at[here], lowered6.at[here], 9, recv_sems.at[7], (above, me)).start()
         pltpu.make_async_copy(out5.at[here, tile(me), :], s5.at[there], own_sems.at[4]).start()
-        pltpu.make_async_copy(out5.at[here], out5_hbm.at[here], out_sems.at[0]).start()
         return carry
 
     lax.fori_loop(0, PARTS, tier_five, 0)
-
+    send_seven(1)
+
+    pltpu.make_async_copy(s5.at[mine], s5.at[mine], own_sems.at[4]).wait()
+    arrived(s5.at[pl.ds(0, total - block)], recv_sems.at[6])
+    prepare(s5.reshape(total * 8, 128), (2, 4), 3)
+    combine(1, 1, sums6)
+    send_home(1, 1, sums6, got6, 0, block)
     own[3].wait()
     arrived(s7.at[pl.ds(0, total - block)], recv_sems.at[2])
     prepare(s7.reshape(total * 8, 128), (0,), 1)
-    pltpu.make_async_copy(s5.at[mine], s5.at[mine], own_sems.at[4]).wait()
-    arrived(s5.at[pl.ds(0, total - block)], recv_sems.at[6])
-    prepare(s5.reshape(total * 8, 128), (2, 4), 3)
-    combine(1, sums6)
-    send_home(1, sums6, got6)
+    combine(1, 0, sums6)
+    send_parts(1, sums6, got6)
     arrived(raised6, recv_sems.at[5])
     arrived(lowered6, recv_sems.at[7])
+    got_home(1, 1, got6, 0, block)
 
     def tier_six(q, carry):
-        got_home(1, sums6, got6, q)
+        got_home(1, 0, got6, q, part)
         for r in range(part):
-            settle(q * part + r, got6, raised6, lowered6, occ6, out6)
-        here = pl.ds(q * part, part)
-        pltpu.make_async_copy(out6.at[here], out6_hbm.at[here], out_sems.at[1]).start()
+            settle(1, q * part + r, got6, raised6, lowered6, out6)
         return carry
 
     lax.fori_loop(0, PARTS, tier_six, 0)
@@ -342,23 +397,12 @@
     sent(tab.at[most], 0)
     sent(s64.at[:, most], 1)
     sent(s7.at[most], 2)
-    for k, copy in enumerate(ring):
+    for copy in ring:
         copy.wait_send()
-    sent(sums5.at[most], 6)
-    sent(sums6.at[most], 7)
+    sent(sums5.at[:, most], 6)
+    sent(sums6.at[:, most], 7)
     sent(s5.at[most], 8)
     sent(lowered6, 9)
-    pltpu.make_async_copy(out5, out5_hbm, out_sems.at[0]).wait()
-    pltpu.make_async_copy(out6, out6_hbm, out_sems.at[1]).wait()
-
-
-def table_of(local, peers, places, occupation, block):
-    base = lax.axis_index("mb").astype(jnp.int32) * block
-    remote = peers * block + places
-    near = local + base
-    return jnp.concatenate(
-        [remote[:, :2], near[:, 0], remote[:, 2:], near[:, 1], occupation[:, 1:]], axis=1
-    )
 
 
 def body(
@@ -384,30 +428,36 @@
     block = tier_four.shape[0]
     total = peers * block
     shape = tier_four.shape
-    table = jnp.concatenate(
-        [
-            jnp.pad(table_of(local_five, peers_five, places_five, occupation_five, block), ((0, 0), (0, 31))),
-            jnp.pad(table_of(local_six, peers_six, places_six, occupation_six, block), ((0, 0), (0, 31))),
-        ],
-        axis=1,
+    flat = (block, 256, 128)
+    hbm = pl.BlockSpec(memory_space=pltpu.HBM)
+    small = (
+        coupling,
+        eigenbasis,
+        energies.reshape(1, -1),
+        decay_rates.reshape(1, -1),
+        bath_coefficients,
+        occupation_five,
+        local_five,
+        peers_five.T,
+        places_five.T,
+        occupation_six,
+        local_six,
+        peers_six.T,
+        places_six.T,
     )
-    flat = (block, 256, 128)
-    any_space = pl.BlockSpec(memory_space=pl.ANY)
-    vmem = pl.BlockSpec(memory_space=pltpu.VMEM)
-    smem = pl.BlockSpec(memory_space=pltpu.SMEM)
-    out = jax.ShapeDtypeStruct(flat, F32)
     store = pltpu.VMEM((total, 8, 128), F32)
-    sums = pltpu.VMEM((total, 2, 8, 128), F32)
-    got = pltpu.VMEM((block, 2, 256, 128), F32)
+    sums = pltpu.VMEM((2, total, 8, 128), F32)
+    got = pltpu.VMEM((2, block, 256, 128), F32)
     whole = pltpu.VMEM(flat, F32)
     dma = pltpu.SemaphoreType.DMA
     five, six = pl.pallas_call(
         functools.partial(sweep_kernel, peers, rows, block),
-        out_shape=(out, out),
-        in_specs=[any_space] * 3 + [vmem] * 4 + [smem] * 4,
-        out_specs=(any_space, any_space),
-        scratch_shapes=[
-            pltpu.VMEM((total, 128), jnp.int32),
+        out_shape=(pltpu.VMEM(flat, F32), pltpu.VMEM(flat, F32)),
+        in_specs=[hbm] * 16,
+        scratch_shapes=[pltpu.VMEM(a.shape, a.dtype) for a in small]
+        + [
+            pltpu.VMEM((block, 128), F32),
+            pltpu.VMEM((total, 128), F32),
             pltpu.VMEM((2, total, 8, 128), F32),
             store,
             store,
@@ -419,36 +469,28 @@
             whole,
             whole,
             whole,
-            whole,
-            whole,
             pltpu.VMEM((2, 2, total, 5 * total), BF16),
             pltpu.VMEM((5 * total, 1024), BF16),
             pltpu.VMEM((6, 128, 128), BF16),
             pltpu.VMEM((2, 128, 256), BF16),
             pltpu.VMEM((2, 128, 128), F32),
+            pltpu.VMEM((2, 3, block, 128), F32),
             dma((10,)),
             dma((8,)),
             dma((5,)),
-            dma((2, PARTS)),
-            dma((2, PARTS)),
-            dma((2,)),
+            dma((2, PARTS + 1)),
+            dma((2, PARTS + 1)),
+            dma((13,)),
         ],
         compiler_params=pltpu.CompilerParams(
-            collective_id=0, has_side_effects=True, vmem_limit_bytes=60 * 1024 * 1024
+            collective_id=0, has_side_effects=True, vmem_limit_bytes=64946176
         ),
         name="sweep",
     )(
         tier_four.reshape(flat),
         tier_six.reshape(flat),
         tier_seven.reshape(flat),
-        table,
-        coupling,
-        eigenbasis,
-        energies.reshape(1, -1),
-        occupation_five,
-        occupation_six,
-        decay_rates,
-        bath_coefficients,
+        *small,
     )
     return five.reshape(shape), six.reshape(shape)
 

time: 123 us -> 109 us (0.89)
  local copies, waits for them, and re-layouts: 8.62 us -> 1.94 us
  Pallas kernels: 112 us -> 106 us
    unnamed x24 -> x2, local copies, waits for them, and re-layouts: 8.16 us -> 1.94 us
    pallas_call x1, Pallas kernels: 112 us -> 106 us  [body(): pl.pallas_call(functools.partial(sweep_kernel, peers, rows, block), out_s...]
where the time goes in v2:
time: 109 us
  Pallas kernels  106 us (97%)
  local copies, waits for them, and re-layouts  1.94 us (2%)
    pallas_call x1, Pallas kernels, body(): pl.pallas_call(functools.partial(sweep_kernel, peers, rows, block), out_s...  106 us

profile of v2, /device:TPU:1, one launch (start us, length us, event | category | flops | bytes accessed | tf_op | source)
XLA Modules:
  0.0 108.8 jit_solution(8058777119817178566)
XLA Ops:
  0.6 106.2 %sweep.1 = (f32[8,256,128]{2,1,0:T(8,128)S(1)}, f32[8,256,128]{2,1,0:T(8,128)S(1)}) custom-call(f32[8,256,128]{2,1,0:T(8,128)} %bitcast.13, f32[8,256,128]{2,1,0:T(8,128)} %bitcast.14, f32[8,256,128]{2,1,0:T(8,128)} %bitcast.15, f32[128,128]{1,0:T(8,128)} %refs_0_.1, f32[128,128]{1,0:T(8,128)} %refs_1_.1, f32[1,128]{1,0:T(1,128)} %bitcast.20, ...), custom_call_target="tpu_custom_call" | custom-call | tf_op jit(solution)/shard_map/sweep/pallas_call | solution.py:453
  106.9 1.0 copy.20
  107.8 1.0 copy.21

commit v3 on v2

v3 whole, which is shorter than its diff:
```python
import functools

import jax
import jax.numpy as jnp
from jax import lax
from jax.experimental import pallas as pl
from jax.experimental.pallas import tpu as pltpu
from jax.sharding import PartitionSpec as P

MESH = pl.DeviceIdType.MESH
F32, BF16 = jnp.float32, jnp.bfloat16
PARTS = 4
STRIDE = 11
LOWER_AT, REAL_AT, IMAG_AT, DAMP_AT, TIER_AT = 11, 22, 34, 46, 64
N_SMALL = 13


def halves(x):
    high = x.astype(BF16)
    return high, (x - high.astype(F32)).astype(BF16)


def mxu(a, b):
    return jnp.dot(a, b, preferred_element_type=F32)


def dot3(a, b):
    return mxu(a[0], b[0]) + (mxu(a[0], b[1]) + mxu(a[1], b[0]))


def beside(x):
    return jnp.concatenate([x[0:128], x[128:256]], axis=1)


EVEN, ODD = pl.ds(0, 128, stride=2), pl.ds(1, 128, stride=2)


def sweep_kernel(peers, rows, block, x4, x6, x7, *refs):
    small, refs = refs[:N_SMALL], refs[N_SMALL:]
    out5, out6, *refs = refs
    local, refs = refs[:N_SMALL], refs[N_SMALL:]
    run(peers, rows, block, (x4, x6, x7), small, local, out5, out6, *refs)


def run(
    peers,
    rows,
    block,
    tiers,
    small,
    local,
    out5,
    out6,
    tab_in,
    tab,
    tab_above,
    held,
    d6,
    ds4,
    d7,
    p5,
    sd6,
    sds4,
    sd7,
    sp5,
    m4,
    m4y,
    d6y,
    d7y,
    y5,
    got5,
    got6,
    sums5,
    sums6,
    drive,
    solved,
    turned_by,
    z6,
    above_weights,
    damp_all,
    weights,
    stack,
    wide,
    both_right,
    split_sq,
    rates,
    send_sems,
    recv_sems,
    part_sems,
    own_sems,
    own_parts,
    small_sems,
):
    total = peers * block
    part = block // PARTS
    rows_part = part * peers
    ma, me = lax.axis_index("ma"), lax.axis_index("mb")
    above = lax.rem(ma + 1, rows)
    below = lax.rem(ma + rows - 1, rows)

    def each_peer(fn):
        def step(j, carry):
            fn(lax.rem(me + lax.rem(j * STRIDE, peers), peers))
            return carry

        lax.fori_loop(1, peers, step, 0)

    def tile(d):
        return pl.ds(pl.multiple_of(d * 8, 8), 8)

    def chunk(q):
        return pl.ds(pl.multiple_of(q * part, part), part)

    others = pl.ds(0, peers - 1)

    def remote(src, dst, k, recv, device):
        return pltpu.make_async_remote_copy(
            src_ref=src,
            dst_ref=dst,
            send_sem=send_sems.at[k],
            recv_sem=recv,
            device_id=device,
            device_id_type=MESH,
        )

    def arrived(ref, recv):
        remote(ref, ref, 0, recv, (above, me)).wait_recv()

    def sent(ref, k):
        remote(ref, ref, k, recv_sems.at[0], (above, me)).wait_send()

    def here(ref, sem):
        pltpu.make_async_copy(ref, ref, sem).wait()

    def flat(ref):
        return ref.reshape(total * 8, 128)

    fetch = [
        pltpu.make_async_copy(a, b, small_sems.at[i]) for i, (a, b) in enumerate(zip(small, local))
    ]
    for copy in fetch:
        copy.start()
    load = [pltpu.make_async_copy(a, held.at[i], own_sems.at[1 + i]) for i, a in enumerate(tiers)]
    for i in (1, 0, 2):
        load[i].start()
    coupling, basis, energies, decay, bath, *tables = local

    barrier = pltpu.get_barrier_semaphore()
    each_peer(lambda d: pl.semaphore_signal(barrier, inc=1, device_id=(ma, d), device_id_type=MESH))
    pl.semaphore_signal(barrier, inc=1, device_id=(above, me), device_id_type=MESH)
    pl.semaphore_signal(barrier, inc=1, device_id=(below, me), device_id_type=MESH)

    for copy in fetch:
        copy.wait()
    lane = lax.broadcasted_iota(jnp.int32, (block, 128), 1)
    on_diagonal = lax.broadcasted_iota(jnp.int32, (block, block), 0) == lax.broadcasted_iota(
        jnp.int32, (block, block), 1
    )
    entries = jnp.zeros((block, 128), F32)

    def put(entries, at, column):
        return jnp.where(lane == at, jnp.broadcast_to(column, (block, 128)), entries)

    for tier in range(2):
        occupation, near, peer_ids, places = tables[4 * tier : 4 * tier + 4]
        base = tier * TIER_AT
        wanted = (places[...] * peers + peer_ids[...]).astype(F32)
        for k in range(4):
            row = jnp.broadcast_to(wanted[k : k + 1, :], (block, block))
            column = jnp.sum(jnp.where(on_diagonal, row, 0.0), axis=1, keepdims=True)
            entries = put(entries, base + (k if k < 2 else LOWER_AT + k - 2), column)
        inside = (near[...] * peers + me).astype(F32)
        up, low = inside[:, 0, :], inside[:, 1, :]
        for k in range(9):
            entries = put(entries, base + 2 + k, up[:, k : k + 1])
            entries = put(entries, base + LOWER_AT + 2 + k, low[:, k : k + 1])
        counted = occupation[...].astype(F32)
        real = counted * bath[0:1, :]
        imag = counted * bath[1:2, :]
        for k in range(12):
            entries = put(entries, base + REAL_AT + k, real[:, k : k + 1])
            entries = put(entries, base + IMAG_AT + k, imag[:, k : k + 1])
        damp = jnp.sum(counted * decay[...], axis=1, keepdims=True)
        entries = put(entries, base + DAMP_AT, damp)
    for spot, column in enumerate((real[:, 0:1], imag[:, 0:1], damp)):
        rates[spot] = jnp.broadcast_to(column, (block, 128))
    tab_in[...] = entries
    mine = pl.ds(pl.multiple_of(me * block, block), block)
    own_tab = pltpu.make_async_copy(tab_in, tab.at[mine], own_sems.at[0])
    own_tab.start()

    e = basis[...]
    turned = jnp.transpose(e)
    e2, c2, t2 = halves(e), halves(coupling[...]), halves(turned)
    wide[0], wide[1] = e2
    wide[2], wide[3] = t2
    ce = halves(dot3(c2, e2))
    wide[4], wide[5] = halves(dot3(t2, ce))
    wide[6], wide[7] = halves(dot3(t2, c2))
    for i in range(2):
        both_right[i, :, 0:128] = e2[i]
        both_right[i, :, 128:256] = ce[i]
    across = jnp.broadcast_to(energies[...], (128, 128))
    split = jnp.transpose(across) - across
    split_sq[0] = split
    split_sq[1] = split * split

    def const(k):
        return wide[2 * k], wide[2 * k + 1]

    basis_at, turned_at, coupled_at, from_left_at = 0, 1, 2, 3

    def products(x):
        t = dot3(halves(x), (both_right[0], both_right[1]))
        left = dot3(const(from_left_at), halves(beside(t[:, 0:128])))
        right = dot3(const(turned_at), halves(beside(t[:, 128:256])))
        return left, right

    def put_commutator(ref, p, q):
        c = p - q
        ref[EVEN, :] = -c[:, 128:256]
        ref[ODD, :] = c[:, 0:128]

    def commutators(which, out, first, count):
        def step(m, carry):
            p, q = products(held[which, m])
            put_commutator(out.at[m], p, q)
            return carry

        lax.fori_loop(first, first + count, step, 0)

    def scatter(src, dst, k, recv, some):
        def fn(d):
            remote(src.at[some, tile(d), :], dst.at[some, me], k, recv, (ma, d)).start()

        each_peer(fn)

    half = block // 2
    load[1].wait()
    commutators(1, d6, 0, half)
    pl.semaphore_wait(barrier, peers + 1)
    each_peer(lambda d: remote(tab_in, tab.at[mine], 0, recv_sems.at[0], (ma, d)).start())
    scatter(d6, sd6, 1, recv_sems.at[1], pl.ds(0, half))
    commutators(1, d6, half, half)
    scatter(d6, sd6, 1, recv_sems.at[1], pl.ds(half, half))
    everything = pl.ds(0, block)
    pltpu.make_async_copy(d6.at[:, tile(me), :], sd6.at[:, me], own_sems.at[4]).start()

    load[0].wait()

    def tier_four(q, carry):
        for r in range(part):
            m = q * part + r
            p, s = products(held[0, m])
            put_commutator(ds4.at[0, m], p, s)
            both = p + s
            ds4[1, m, EVEN, :] = both[:, 0:128]
            ds4[1, m, ODD, :] = both[:, 128:256]

        def fn(d):
            remote(
                ds4.at[:, chunk(q), tile(d), :],
                sds4.at[:, chunk(q), me],
                2,
                part_sems.at[0, q],
                (ma, d),
            ).start()

        each_peer(fn)
        pltpu.make_async_copy(
            ds4.at[:, chunk(q), tile(me), :], sds4.at[:, chunk(q), me], own_parts.at[0, q]
        ).start()
        return carry

    lax.fori_loop(0, PARTS, tier_four, 0)

    load[2].wait()
    commutators(2, d7, 0, block)
    scatter(d7, sd7, 3, recv_sems.at[2], everything)
    pltpu.make_async_copy(d7.at[:, tile(me), :], sd7.at[:, me], own_sems.at[5]).start()

    own_tab.wait()
    arrived(tab.at[pl.ds(0, total - block)], recv_sems.at[0])
    remote(tab, tab_above, 4, recv_sems.at[3], (below, me)).start()
    here(sd6.at[:, me], own_sems.at[4])
    arrived(sd6.at[:, others], recv_sems.at[1])
    remote(sd6, d6y, 5, recv_sems.at[4], (below, me)).start()
    remote(d7, d7y, 6, recv_sems.at[5], (below, me)).start()

    def weigh(tier):
        base = tier * TIER_AT

        def step(i, carry):
            at = pl.ds(pl.multiple_of(i * peers, peers), peers)
            t = tab[pl.ds(i, peers, stride=block), :]
            column = lax.broadcasted_iota(jnp.int32, (peers, total), 1).astype(F32)
            up = jnp.zeros((peers, total), F32)
            real = jnp.zeros((peers, total), F32)
            imag = jnp.zeros((peers, total), F32)
            for k in range(11):
                hit = t[:, base + k : base + k + 1] == column
                up = up + jnp.where(hit, 1.0, 0.0)
                hit = t[:, base + LOWER_AT + k : base + LOWER_AT + k + 1] == column
                wr = t[:, base + REAL_AT + k + 1 : base + REAL_AT + k + 2]
                wi = t[:, base + IMAG_AT + k + 1 : base + IMAG_AT + k + 2]
                real = real + jnp.where(hit, wr, 0.0)
                imag = imag - jnp.where(hit, wi, 0.0)
            rh, rl = halves(real)
            ih, il = halves(imag)
            u = up.astype(BF16)
            for spot, value in enumerate((u, u, rh, rh, rl, ih, ih, il)):
                weights[tier, at, spot * total : (spot + 1) * total] = value
            if tier == 0:
                damp_all[at, :] = jnp.broadcast_to(t[:, DAMP_AT : DAMP_AT + 1], (peers, 128))
            return carry

        lax.fori_loop(0, block, step, 0)

    weigh(0)
    arrived(tab_above, recv_sems.at[3])

    def next_row(i, carry):
        at = pl.ds(pl.multiple_of(i * peers, peers), peers)
        t = tab_above[pl.ds(i, peers, stride=block), :]
        above_weights[0, at, :] = jnp.broadcast_to(t[:, REAL_AT : REAL_AT + 1], (peers, 128))
        above_weights[1, at, :] = jnp.broadcast_to(t[:, IMAG_AT : IMAG_AT + 1], (peers, 128))
        return carry

    lax.fori_loop(0, block, next_row, 0)

    def store_halves(at, lanes, value, spots_high, spot_low):
        high, low = halves(value)
        for spot in spots_high:
            stack[pl.ds(at + spot * total, value.shape[0]), lanes] = high
        stack[pl.ds(at + spot_low * total, value.shape[0]), lanes] = low

    def lanes_of(s):
        return slice(128 * s, 128 * s + 128)

    def prepare(store):
        for s in range(8):
            store_halves(0, lanes_of(s), flat(store)[pl.ds(s, total, stride=8), :], (0,), 1)

    prepare(sd6)
    weigh(1)

    def tier_four_came(q, carry):
        here(sds4.at[:, chunk(q), me], own_parts.at[0, q])
        arrived(sds4.at[:, chunk(q), others], part_sems.at[0, q])
        at = pl.multiple_of(q * rows_part, rows_part)
        wr = above_weights[0, pl.ds(at, rows_part), :]
        wi = above_weights[1, pl.ds(at, rows_part), :]
        for s in range(8):
            spread = pl.ds(at * 8 + s, rows_part, stride=8)
            c = flat(sds4.at[0])[spread, :]
            a = flat(sds4.at[1])[spread, :]
            flat(m4)[spread, :] = wr * c - wi * a
            store_halves(at, lanes_of(s), c, (2, 4), 3)
            store_halves(at, lanes_of(s), a, (5, 7), 6)
        remote(m4.at[chunk(q)], m4y.at[chunk(q)], 7, part_sems.at[1, q], (above, me)).start()
        return carry

    lax.fori_loop(0, PARTS, tier_four_came, 0)

    def combine(tier, store):
        for pair in range(4):
            lanes = slice(256 * pair, 256 * pair + 256)
            a = mxu(weights[tier], stack[:, lanes])
            for t in range(2):
                store(2 * pair + t, a[:, 128 * t : 128 * t + 128])

    def keep(s, value):
        drive[s] = value

    combine(0, keep)

    def send_home(sums, got, q, k, row):
        pltpu.make_async_copy(
            sums.at[chunk(q), me], got.at[chunk(q), tile(me), :], own_parts.at[row - 1, q]
        ).start()

        def fn(d):
            remote(
                sums.at[chunk(q), d],
                got.at[chunk(q), tile(me), :],
                k,
                part_sems.at[row, q],
                (ma, d),
            ).start()

        each_peer(fn)

    def got_home(got, q, row):
        here(got.at[chunk(q), tile(me), :], own_parts.at[row - 1, q])
        arrived(got.at[chunk(q), pl.ds(0, 8 * (peers - 1)), :], part_sems.at[row, q])

    arrived(d6y, recv_sems.at[4])

    def solve_five(q, carry):
        arrived(m4y.at[chunk(q)], part_sems.at[1, q])
        at = pl.multiple_of(q * rows_part, rows_part)
        some = pl.ds(at, rows_part)
        damping = damp_all[some, :]
        for t in range(4):
            gap = split_sq[0, pl.ds(me * 4 + t, 1), :]
            inverse = 1.0 / (damping * damping + gap * gap)
            factor_real = -damping * inverse
            factor_imag = gap * inverse
            value = []
            for s in (2 * t, 2 * t + 1):
                spread = pl.ds(at * 8 + s, rows_part, stride=8)
                value.append(drive[s, some, :] + flat(d6y)[spread, :] + flat(m4y)[spread, :])
            real = value[0] * factor_real - value[1] * factor_imag
            imag = value[0] * factor_imag + value[1] * factor_real
            for s, v in ((2 * t, real), (2 * t + 1, imag)):
                solved[s, some, :] = v
                flat(sums5)[pl.ds(at * 8 + s, rows_part, stride=8), :] = v
        send_home(sums5, got5, q, 8, 2)
        return carry

    lax.fori_loop(0, PARTS, solve_five, 0)

    def turn(s, carry):
        turned_by[s] = dot3(halves(solved[s]), const(coupled_at))
        return carry

    lax.fori_loop(0, 8, turn, 0)

    def whole(real, imag):
        y = jnp.concatenate([real, imag], axis=0)
        return dot3(const(basis_at), halves(beside(dot3(halves(y), const(turned_at)))))

    def tier_five(q, carry):
        got_home(got5, q, 2)
        remote(got5.at[chunk(q)], y5.at[chunk(q)], 9, part_sems.at[4, q], (above, me)).start()
        for r in range(part):
            m = q * part + r
            y = jnp.concatenate([got5[m, EVEN, :], got5[m, ODD, :]], axis=1)
            p = dot3(const(coupled_at), halves(y))
            p5[m, EVEN, :] = p[:, 0:128]
            p5[m, ODD, :] = p[:, 128:256]
        scatter(p5, sp5, 10, recv_sems.at[6], chunk(q))
        pltpu.make_async_copy(
            p5.at[chunk(q), tile(me), :], sp5.at[chunk(q), me], own_sems.at[6]
        ).start()
        for r in range(part):
            m = q * part + r
            back = whole(got5[m, EVEN, :], got5[m, ODD, :])
            out5[m, 0:128, :] = back[:, 0:128]
            out5[m, 128:256, :] = back[:, 128:256]
        return carry

    lax.fori_loop(0, PARTS, tier_five, 0)

    here(sd7.at[:, me], own_sems.at[5])
    arrived(sd7.at[:, others], recv_sems.at[2])
    prepare(sd7)
    here(sp5.at[:, me], own_sems.at[6])
    arrived(sp5.at[:, others], recv_sems.at[6])
    for t in range(4):
        p = [flat(sp5)[pl.ds(s, total, stride=8), :] for s in (2 * t, 2 * t + 1)]
        q = [turned_by[s] for s in (2 * t, 2 * t + 1)]
        store_halves(0, lanes_of(2 * t), q[1] - p[1], (2, 4), 3)
        store_halves(0, lanes_of(2 * t + 1), p[0] - q[0], (2, 4), 3)
        store_halves(0, lanes_of(2 * t), p[0] + q[0], (5, 7), 6)
        store_halves(0, lanes_of(2 * t + 1), p[1] + q[1], (5, 7), 6)

    def spread_out(s, value):
        flat(sums6)[pl.ds(s, total, stride=8), :] = value

    combine(1, spread_out)

    def home_six(q, carry):
        send_home(sums6, got6, q, 11, 3)
        return carry

    lax.fori_loop(0, PARTS, home_six, 0)

    arrived(d7y, recv_sems.at[5])

    def first_mode(q, carry):
        arrived(y5.at[chunk(q)], part_sems.at[4, q])
        for r in range(part):
            m = q * part + r
            real, imag = y5[m, EVEN, :], y5[m, ODD, :]
            p = dot3(const(coupled_at), halves(jnp.concatenate([real, imag], axis=1)))
            s = beside(
                dot3(halves(jnp.concatenate([real, imag], axis=0)), const(coupled_at))
            )
            c, a = p - s, p + s
            wr = rates[0, pl.ds(m, 1), :]
            wi = rates[1, pl.ds(m, 1), :]
            z6[m, 0:128, :] = d7y[m, EVEN, :] - wr * c[:, 128:256] - wi * a[:, 0:128]
            z6[m, 128:256, :] = d7y[m, ODD, :] + wr * c[:, 0:128] - wi * a[:, 128:256]
        return carry

    lax.fori_loop(0, PARTS, first_mode, 0)

    def tier_six(q, carry):
        got_home(got6, q, 3)
        for r in range(part):
            m = q * part + r
            damping = jnp.broadcast_to(rates[2, pl.ds(m, 1), :], (128, 128))
            inverse = 1.0 / (damping * damping + split_sq[1])
            factor_real = -damping * inverse
            factor_imag = split_sq[0] * inverse
            real = got6[m, EVEN, :] + z6[m, 0:128, :]
            imag = got6[m, ODD, :] + z6[m, 128:256, :]
            back = whole(
                real * factor_real - imag * factor_imag, real * factor_imag + imag * factor_real
            )
            out6[m, 0:128, :] = back[:, 0:128]
            out6[m, 128:256, :] = back[:, 128:256]
        return carry

    lax.fori_loop(0, PARTS, tier_six, 0)

    sent(tab.at[pl.ds(0, total - block)], 0)
    sent(sd6.at[:, others], 1)
    sent(sds4.at[:, :, others], 2)
    sent(sd7.at[:, others], 3)
    sent(tab, 4)
    sent(sd6, 5)
    sent(d7, 6)
    sent(m4, 7)
    sent(sums5.at[:, others], 8)
    sent(got5, 9)
    sent(sp5.at[:, others], 10)
    sent(sums6.at[:, others], 11)


def body(
    rows,
    peers,
    tier_four,
    tier_six,
    tier_seven,
    coupling,
    eigenbasis,
    energies,
    decay_rates,
    bath_coefficients,
    occupation_five,
    local_five,
    peers_five,
    places_five,
    occupation_six,
    local_six,
    peers_six,
    places_six,
):
    block = tier_four.shape[0]
    total = peers * block
    shape = tier_four.shape
    flat = (block, 256, 128)
    hbm = pl.BlockSpec(memory_space=pltpu.HBM)
    small = (
        coupling,
        eigenbasis,
        energies.reshape(1, -1),
        decay_rates.reshape(1, -1),
        bath_coefficients,
        occupation_five,
        local_five,
        peers_five.T,
        places_five.T,
        occupation_six,
        local_six,
        peers_six.T,
        places_six.T,
    )
    whole = pltpu.VMEM(flat, F32)
    pair = pltpu.VMEM((2,) + flat, F32)
    store = pltpu.VMEM((block, peers, 8, 128), F32)
    pair_store = pltpu.VMEM((2, block, peers, 8, 128), F32)
    slices = pltpu.VMEM((8, total, 128), F32)
    table = pltpu.VMEM((total, 128), F32)
    dma = pltpu.SemaphoreType.DMA
    five, six = pl.pallas_call(
        functools.partial(sweep_kernel, peers, rows, block),
        out_shape=(pltpu.VMEM(flat, F32), pltpu.VMEM(flat, F32)),
        in_specs=[hbm] * (3 + len(small)),
        scratch_shapes=[pltpu.VMEM(a.shape, a.dtype) for a in small]
        + [
            pltpu.VMEM((block, 128), F32),
            table,
            table,
            pltpu.VMEM((3,) + flat, F32),
            whole,
            pair,
            whole,
            whole,
            store,
            pair_store,
            store,
            store,
            store,
            store,
            store,
            whole,
            whole,
            whole,
            whole,
            store,
            store,
            slices,
            slices,
            slices,
            whole,
            pltpu.VMEM((2, total, 128), F32),
            table,
            pltpu.VMEM((2, total, 8 * total), BF16),
            pltpu.VMEM((8 * total, 1024), BF16),
            pltpu.VMEM((8, 128, 128), BF16),
            pltpu.VMEM((2, 128, 256), BF16),
            pltpu.VMEM((2, 128, 128), F32),
            pltpu.VMEM((3, block, 128), F32),
            dma((12,)),
            dma((7,)),
            dma((5, PARTS)),
            dma((7,)),
            dma((3, PARTS)),
            dma((N_SMALL,)),
        ],
        compiler_params=pltpu.CompilerParams(
            collective_id=0, has_side_effects=True, vmem_limit_bytes=64946176
        ),
        name="sweep",
    )(
        tier_four.reshape(flat),
        tier_six.reshape(flat),
        tier_seven.reshape(flat),
        *small,
    )
    return five.reshape(shape), six.reshape(shape)


def solution(mesh):
    rows, peers = mesh.shape["ma"], mesh.shape["mb"]
    whole = P(("ma", "mb"), None, None, None)
    wide = P(("ma", "mb"), None)
    tables = (wide, P(("ma", "mb"), None, None), wide, wide)
    in_specs = (whole,) * 3 + (P(),) * 5 + tables + tables
    return jax.shard_map(
        functools.partial(body, rows, peers),
        mesh=mesh,
        in_specs=in_specs,
        out_specs=(whole, whole),
        check_vma=False,
    )
```

time: 109 us -> 100 us (0.917)
  Pallas kernels: 106 us -> 97.8 us
    pallas_call x1, Pallas kernels: 106 us -> 97.8 us  [body(): pl.pallas_call(functools.partial(sweep_kernel, peers, rows, block), out_s...]
where the time goes in v3:
time: 100 us
  Pallas kernels  97.8 us (98%)
  local copies, waits for them, and re-layouts  1.94 us (2%)
    pallas_call x1, Pallas kernels, body(): pl.pallas_call(functools.partial(sweep_kernel, peers, rows, block), out_s...  97.8 us

profile of v3, /device:TPU:1, one launch (start us, length us, event | category | flops | bytes accessed | tf_op | source)
XLA Modules:
  0.0 100.3 jit_solution(13811080500567469575)
XLA Ops:
  0.6 97.8 %sweep.1 = (f32[8,256,128]{2,1,0:T(8,128)S(1)}, f32[8,256,128]{2,1,0:T(8,128)S(1)}) custom-call(f32[8,256,128]{2,1,0:T(8,128)} %bitcast.13, f32[8,256,128]{2,1,0:T(8,128)} %bitcast.14, f32[8,256,128]{2,1,0:T(8,128)} %bitcast.15, f32[128,128]{1,0:T(8,128)} %refs_0_.1, f32[128,128]{1,0:T(8,128)} %refs_1_.1, f32[1,128]{1,0:T(1,128)} %bitcast.20, ...), custom_call_target="tpu_custom_call" | custom-call | tf_op jit(solution)/shard_map/sweep/pallas_call | solution.py:579
  98.4 1.0 copy.20
  99.4 1.0 copy.21

commit v4 on v3

--- a/solution.py
+++ b/solution.py
@@ -57,16 +57,14 @@
     held,
     d6,
     ds4,
-    d7,
-    p5,
+    x7,
     sd6,
     sds4,
-    sd7,
-    sp5,
+    sx7,
     m4,
     m4y,
     d6y,
-    d7y,
+    x7y,
     y5,
     got5,
     got6,
@@ -74,7 +72,6 @@
     sums6,
     drive,
     solved,
-    turned_by,
     z6,
     above_weights,
     damp_all,
@@ -89,6 +86,8 @@
     part_sems,
     own_sems,
     own_parts,
+    home_recv,
+    home_own,
     small_sems,
 ):
     total = peers * block
@@ -135,6 +134,11 @@
     def flat(ref):
         return ref.reshape(total * 8, 128)
 
+    barrier = pltpu.get_barrier_semaphore()
+    each_peer(lambda d: pl.semaphore_signal(barrier, inc=1, device_id=(ma, d), device_id_type=MESH))
+    pl.semaphore_signal(barrier, inc=1, device_id=(above, me), device_id_type=MESH)
+    pl.semaphore_signal(barrier, inc=1, device_id=(below, me), device_id_type=MESH)
+
     fetch = [
         pltpu.make_async_copy(a, b, small_sems.at[i]) for i, (a, b) in enumerate(zip(small, local))
     ]
@@ -144,11 +148,6 @@
     for i in (1, 0, 2):
         load[i].start()
     coupling, basis, energies, decay, bath, *tables = local
-
-    barrier = pltpu.get_barrier_semaphore()
-    each_peer(lambda d: pl.semaphore_signal(barrier, inc=1, device_id=(ma, d), device_id_type=MESH))
-    pl.semaphore_signal(barrier, inc=1, device_id=(above, me), device_id_type=MESH)
-    pl.semaphore_signal(barrier, inc=1, device_id=(below, me), device_id_type=MESH)
 
     for copy in fetch:
         copy.wait()
@@ -275,9 +274,17 @@
     lax.fori_loop(0, PARTS, tier_four, 0)
 
     load[2].wait()
-    commutators(2, d7, 0, block)
-    scatter(d7, sd7, 3, recv_sems.at[2], everything)
-    pltpu.make_async_copy(d7.at[:, tile(me), :], sd7.at[:, me], own_sems.at[5]).start()
+
+    def tier_seven(m, carry):
+        t = beside(dot3(halves(held[2, m]), const(basis_at)))
+        x = dot3(const(turned_at), halves(t))
+        x7[m, EVEN, :] = x[:, 0:128]
+        x7[m, ODD, :] = x[:, 128:256]
+        return carry
+
+    lax.fori_loop(0, block, tier_seven, 0)
+    scatter(x7, sx7, 3, recv_sems.at[2], everything)
+    pltpu.make_async_copy(x7.at[:, tile(me), :], sx7.at[:, me], own_sems.at[5]).start()
 
     own_tab.wait()
     arrived(tab.at[pl.ds(0, total - block)], recv_sems.at[0])
@@ -285,7 +292,7 @@
     here(sd6.at[:, me], own_sems.at[4])
     arrived(sd6.at[:, others], recv_sems.at[1])
     remote(sd6, d6y, 5, recv_sems.at[4], (below, me)).start()
-    remote(d7, d7y, 6, recv_sems.at[5], (below, me)).start()
+    remote(x7, x7y, 6, recv_sems.at[5], (below, me)).start()
 
     def weigh(tier):
         base = tier * TIER_AT
@@ -304,9 +311,9 @@
                 wr = t[:, base + REAL_AT + k + 1 : base + REAL_AT + k + 2]
                 wi = t[:, base + IMAG_AT + k + 1 : base + IMAG_AT + k + 2]
                 real = real + jnp.where(hit, wr, 0.0)
-                imag = imag - jnp.where(hit, wi, 0.0)
+                imag = imag + jnp.where(hit, wi, 0.0)
             rh, rl = halves(real)
-            ih, il = halves(imag)
+            ih, il = halves(-imag if tier == 0 else imag)
             u = up.astype(BF16)
             for spot, value in enumerate((u, u, rh, rh, rl, ih, ih, il)):
                 weights[tier, at, spot * total : (spot + 1) * total] = value
@@ -362,37 +369,25 @@
 
     lax.fori_loop(0, PARTS, tier_four_came, 0)
 
-    def combine(tier, store):
-        for pair in range(4):
-            lanes = slice(256 * pair, 256 * pair + 256)
-            a = mxu(weights[tier], stack[:, lanes])
-            for t in range(2):
-                store(2 * pair + t, a[:, 128 * t : 128 * t + 128])
-
-    def keep(s, value):
-        drive[s] = value
-
-    combine(0, keep)
-
-    def send_home(sums, got, q, k, row):
-        pltpu.make_async_copy(
-            sums.at[chunk(q), me], got.at[chunk(q), tile(me), :], own_parts.at[row - 1, q]
-        ).start()
+    def lanes_of_pair(pair):
+        return slice(256 * pair, 256 * pair + 256)
+
+    for pair in range(4):
+        a = mxu(weights[0], stack[:, lanes_of_pair(pair)])
+        drive[2 * pair] = a[:, 0:128]
+        drive[2 * pair + 1] = a[:, 128:256]
+
+    def send_home(src_of, got, where, k, own, recv):
+        pltpu.make_async_copy(src_of(me), got.at[where + (tile(me),)], own).start()
 
         def fn(d):
-            remote(
-                sums.at[chunk(q), d],
-                got.at[chunk(q), tile(me), :],
-                k,
-                part_sems.at[row, q],
-                (ma, d),
-            ).start()
+            remote(src_of(d), got.at[where + (tile(me),)], k, recv, (ma, d)).start()
 
         each_peer(fn)
 
-    def got_home(got, q, row):
-        here(got.at[chunk(q), tile(me), :], own_parts.at[row - 1, q])
-        arrived(got.at[chunk(q), pl.ds(0, 8 * (peers - 1)), :], part_sems.at[row, q])
+    def got_home(got, where, own, recv):
+        here(got.at[where + (tile(me),)], own)
+        arrived(got.at[where + (pl.ds(0, 8 * (peers - 1)),)], recv)
 
     arrived(d6y, recv_sems.at[4])
 
@@ -415,34 +410,55 @@
             for s, v in ((2 * t, real), (2 * t + 1, imag)):
                 solved[s, some, :] = v
                 flat(sums5)[pl.ds(at * 8 + s, rows_part, stride=8), :] = v
-        send_home(sums5, got5, q, 8, 2)
+        send_home(
+            lambda d: sums5.at[chunk(q), d],
+            got5,
+            (chunk(q),),
+            8,
+            own_parts.at[1, q],
+            part_sems.at[2, q],
+        )
         return carry
 
     lax.fori_loop(0, PARTS, solve_five, 0)
-
-    def turn(s, carry):
-        turned_by[s] = dot3(halves(solved[s]), const(coupled_at))
-        return carry
-
-    lax.fori_loop(0, 8, turn, 0)
 
     def whole(real, imag):
         y = jnp.concatenate([real, imag], axis=0)
         return dot3(const(basis_at), halves(beside(dot3(halves(y), const(turned_at)))))
 
+    here(sx7.at[:, me], own_sems.at[5])
+    arrived(sx7.at[:, others], recv_sems.at[2])
+    prepare(sx7)
+    for s in range(8):
+        store_halves(0, lanes_of(s), solved[s], (2, 4), 3)
+    for t in range(4):
+        a = mxu(weights[1, :, 0 : 5 * total], stack[0 : 5 * total, lanes_of_pair(t)])
+        b = mxu(weights[1, :, 5 * total :], stack[2 * total : 5 * total, lanes_of_pair(t)])
+        ar, ai, br, bi = a[:, 0:128], a[:, 128:256], b[:, 0:128], b[:, 128:256]
+        other = dot3(
+            halves(jnp.concatenate([ar + bi, ai - br], axis=0)), const(coupled_at)
+        )
+        for r, value in enumerate((ar - bi, ai + br)):
+            spread = pl.ds(2 * t + r, total, stride=8)
+            flat(sums6.at[0])[spread, :] = value
+            flat(sums6.at[1])[spread, :] = other[r * total : (r + 1) * total]
+
+    def home_six(q, carry):
+        send_home(
+            lambda d: sums6.at[:, q, d],
+            got6,
+            (slice(None), q),
+            10,
+            home_own.at[q],
+            home_recv.at[q],
+        )
+        return carry
+
+    lax.fori_loop(0, block, home_six, 0)
+
     def tier_five(q, carry):
-        got_home(got5, q, 2)
-        remote(got5.at[chunk(q)], y5.at[chunk(q)], 9, part_sems.at[4, q], (above, me)).start()
-        for r in range(part):
-            m = q * part + r
-            y = jnp.concatenate([got5[m, EVEN, :], got5[m, ODD, :]], axis=1)
-            p = dot3(const(coupled_at), halves(y))
-            p5[m, EVEN, :] = p[:, 0:128]
-            p5[m, ODD, :] = p[:, 128:256]
-        scatter(p5, sp5, 10, recv_sems.at[6], chunk(q))
-        pltpu.make_async_copy(
-            p5.at[chunk(q), tile(me), :], sp5.at[chunk(q), me], own_sems.at[6]
-        ).start()
+        got_home(got5, (chunk(q),), own_parts.at[1, q], part_sems.at[2, q])
+        remote(got5.at[chunk(q)], y5.at[chunk(q)], 9, part_sems.at[3, q], (above, me)).start()
         for r in range(part):
             m = q * part + r
             back = whole(got5[m, EVEN, :], got5[m, ODD, :])
@@ -452,81 +468,61 @@
 
     lax.fori_loop(0, PARTS, tier_five, 0)
 
-    here(sd7.at[:, me], own_sems.at[5])
-    arrived(sd7.at[:, others], recv_sems.at[2])
-    prepare(sd7)
-    here(sp5.at[:, me], own_sems.at[6])
-    arrived(sp5.at[:, others], recv_sems.at[6])
-    for t in range(4):
-        p = [flat(sp5)[pl.ds(s, total, stride=8), :] for s in (2 * t, 2 * t + 1)]
-        q = [turned_by[s] for s in (2 * t, 2 * t + 1)]
-        store_halves(0, lanes_of(2 * t), q[1] - p[1], (2, 4), 3)
-        store_halves(0, lanes_of(2 * t + 1), p[0] - q[0], (2, 4), 3)
-        store_halves(0, lanes_of(2 * t), p[0] + q[0], (5, 7), 6)
-        store_halves(0, lanes_of(2 * t + 1), p[1] + q[1], (5, 7), 6)
-
-    def spread_out(s, value):
-        flat(sums6)[pl.ds(s, total, stride=8), :] = value
-
-    combine(1, spread_out)
-
-    def home_six(q, carry):
-        send_home(sums6, got6, q, 11, 3)
-        return carry
-
-    lax.fori_loop(0, PARTS, home_six, 0)
-
-    arrived(d7y, recv_sems.at[5])
-
-    def first_mode(q, carry):
-        arrived(y5.at[chunk(q)], part_sems.at[4, q])
+    arrived(x7y, recv_sems.at[5])
+
+    def first_mode(q):
+        arrived(y5.at[chunk(q)], part_sems.at[3, q])
         for r in range(part):
             m = q * part + r
             real, imag = y5[m, EVEN, :], y5[m, ODD, :]
-            p = dot3(const(coupled_at), halves(jnp.concatenate([real, imag], axis=1)))
-            s = beside(
-                dot3(halves(jnp.concatenate([real, imag], axis=0)), const(coupled_at))
-            )
-            c, a = p - s, p + s
             wr = rates[0, pl.ds(m, 1), :]
             wi = rates[1, pl.ds(m, 1), :]
-            z6[m, 0:128, :] = d7y[m, EVEN, :] - wr * c[:, 128:256] - wi * a[:, 0:128]
-            z6[m, 128:256, :] = d7y[m, ODD, :] + wr * c[:, 0:128] - wi * a[:, 128:256]
-        return carry
-
-    lax.fori_loop(0, PARTS, first_mode, 0)
-
-    def tier_six(q, carry):
-        got_home(got6, q, 3)
+            ar, ai = x7y[m, EVEN, :] + wr * real, x7y[m, ODD, :] + wr * imag
+            br, bi = wi * real, wi * imag
+            z6[0, m] = jnp.concatenate([ar - bi, ai + br], axis=0)
+            z6[1, m] = dot3(
+                halves(jnp.concatenate([ar + bi, ai - br], axis=0)), const(coupled_at)
+            )
+
+    def tier_six(m):
+        got_home(got6, (slice(None), m), home_own.at[m], home_recv.at[m])
+        pair = jnp.concatenate(
+            [got6[0, m, EVEN, :] + z6[0, m, 0:128], got6[0, m, ODD, :] + z6[0, m, 128:256]], axis=1
+        )
+        other = jnp.concatenate(
+            [got6[1, m, EVEN, :] + z6[1, m, 0:128], got6[1, m, ODD, :] + z6[1, m, 128:256]], axis=1
+        )
+        comm = dot3(const(coupled_at), halves(pair)) - other
+        real, imag = -comm[:, 128:256], comm[:, 0:128]
+        damping = jnp.broadcast_to(rates[2, pl.ds(m, 1), :], (128, 128))
+        inverse = 1.0 / (damping * damping + split_sq[1])
+        factor_real = -damping * inverse
+        factor_imag = split_sq[0] * inverse
+        back = whole(
+            real * factor_real - imag * factor_imag, real * factor_imag + imag * factor_real
+        )
+        out6[m, 0:128, :] = back[:, 0:128]
+        out6[m, 128:256, :] = back[:, 128:256]
+
+    def finish(q, carry):
+        first_mode(q)
         for r in range(part):
-            m = q * part + r
-            damping = jnp.broadcast_to(rates[2, pl.ds(m, 1), :], (128, 128))
-            inverse = 1.0 / (damping * damping + split_sq[1])
-            factor_real = -damping * inverse
-            factor_imag = split_sq[0] * inverse
-            real = got6[m, EVEN, :] + z6[m, 0:128, :]
-            imag = got6[m, ODD, :] + z6[m, 128:256, :]
-            back = whole(
-                real * factor_real - imag * factor_imag, real * factor_imag + imag * factor_real
-            )
-            out6[m, 0:128, :] = back[:, 0:128]
-            out6[m, 128:256, :] = back[:, 128:256]
-        return carry
-
-    lax.fori_loop(0, PARTS, tier_six, 0)
+            tier_six(q * part + r)
+        return carry
+
+    lax.fori_loop(0, PARTS, finish, 0)
 
     sent(tab.at[pl.ds(0, total - block)], 0)
     sent(sd6.at[:, others], 1)
     sent(sds4.at[:, :, others], 2)
-    sent(sd7.at[:, others], 3)
+    sent(sx7.at[:, others], 3)
     sent(tab, 4)
     sent(sd6, 5)
-    sent(d7, 6)
+    sent(x7, 6)
     sent(m4, 7)
     sent(sums5.at[:, others], 8)
     sent(got5, 9)
-    sent(sp5.at[:, others], 10)
-    sent(sums6.at[:, others], 11)
+    sent(sums6.at[:, :, others], 10)
 
 
 def body(
@@ -589,10 +585,8 @@
             whole,
             pair,
             whole,
-            whole,
             store,
             pair_store,
-            store,
             store,
             store,
             store,
@@ -600,13 +594,12 @@
             whole,
             whole,
             whole,
-            whole,
+            pair,
             store,
-            store,
+            pair_store,
             slices,
             slices,
-            slices,
-            whole,
+            pair,
             pltpu.VMEM((2, total, 128), F32),
             table,
             pltpu.VMEM((2, total, 8 * total), BF16),
@@ -615,11 +608,13 @@
             pltpu.VMEM((2, 128, 256), BF16),
             pltpu.VMEM((2, 128, 128), F32),
             pltpu.VMEM((3, block, 128), F32),
-            dma((12,)),
-            dma((7,)),
-            dma((5, PARTS)),
-            dma((7,)),
-            dma((3, PARTS)),
+            dma((11,)),
+            dma((6,)),
+            dma((4, PARTS)),
+            dma((6,)),
+            dma((2, PARTS)),
+            dma((block,)),
+            dma((block,)),
             dma((N_SMALL,)),
         ],
         compiler_params=pltpu.CompilerParams(

time: 100 us -> 97.1 us (0.971)
  Pallas kernels: 97.8 us -> 94.3 us
    pallas_call x1, Pallas kernels: 97.8 us -> 94.3 us  [body(): pl.pallas_call(functools.partial(sweep_kernel, peers, rows, block), out_s...]
where the time goes in v4:
time: 97.1 us; the launch traced here: 96.9 us
  Pallas kernels  94.3 us (97%)
  local copies, waits for them, and re-layouts  1.94 us (2%)
    pallas_call x1, Pallas kernels, body(): pl.pallas_call(functools.partial(sweep_kernel, peers, rows, block), out_s...  94.3 us
    unnamed x2, local copies, waits for them, and re-layouts  1.94 us

profile of v4, /device:TPU:1, one launch (start us, length us, event | category | flops | bytes accessed | tf_op | source)
XLA Modules:
  0.0 96.9 jit_solution(14038167216070915010)
XLA Ops:
  0.6 94.3 %sweep.1 = (f32[8,256,128]{2,1,0:T(8,128)S(1)}, f32[8,256,128]{2,1,0:T(8,128)S(1)}) custom-call(f32[8,256,128]{2,1,0:T(8,128)} %bitcast.13, f32[8,256,128]{2,1,0:T(8,128)} %bitcast.14, f32[8,256,128]{2,1,0:T(8,128)} %bitcast.15, f32[128,128]{1,0:T(8,128)} %refs_0_.1, f32[128,128]{1,0:T(8,128)} %refs_1_.1, f32[1,128]{1,0:T(1,128)} %bitcast.20, ...), custom_call_target="tpu_custom_call" | custom-call | tf_op jit(solution)/shard_map/sweep/pallas_call | solution.py:575
  94.9 1.0 %copy.20 = f32[8,2,128,128]{3,2,1,0:T(8,128)} copy(f32[8,2,128,128]{3,2,1,0:T(8,128)S(1)} %bitcast.12) | data formatting | bytes 2097152
  95.9 1.0 %copy.21 = f32[8,2,128,128]{3,2,1,0:T(8,128)} copy(f32[8,2,128,128]{3,2,1,0:T(8,128)S(1)} %bitcast.11) | data formatting | bytes 2097152

commit v5 on v4

--- a/solution.py
+++ b/solution.py
@@ -10,7 +10,7 @@
 MESH = pl.DeviceIdType.MESH
 F32, BF16 = jnp.float32, jnp.bfloat16
 PARTS = 4
-STRIDE = 11
+STRIDE = 5
 LOWER_AT, REAL_AT, IMAG_AT, DAMP_AT, TIER_AT = 11, 22, 34, 46, 64
 N_SMALL = 13
 

time: 97.1 us -> 97.1 us (level)
  no operation moved by 1% of the time
where the time goes in v5:
time: 97.1 us; the launch traced here: 97 us
  Pallas kernels  94.4 us (97%)
  local copies, waits for them, and re-layouts  1.94 us (2%)
    pallas_call x1, Pallas kernels, body(): pl.pallas_call(functools.partial(sweep_kernel, peers, rows, block), out_s...  94.4 us
    unnamed x2, local copies, waits for them, and re-layouts  1.94 us

profile of v5, /device:TPU:1, one launch (start us, length us, event | category | flops | bytes accessed | tf_op | source)
XLA Modules:
  0.0 97.0 jit_solution(15848365505010260926)
XLA Ops:
  0.6 94.4 %sweep.1 = (f32[8,256,128]{2,1,0:T(8,128)S(1)}, f32[8,256,128]{2,1,0:T(8,128)S(1)}) custom-call(f32[8,256,128]{2,1,0:T(8,128)} %bitcast.13, f32[8,256,128]{2,1,0:T(8,128)} %bitcast.14, f32[8,256,128]{2,1,0:T(8,128)} %bitcast.15, f32[128,128]{1,0:T(8,128)} %refs_0_.1, f32[128,128]{1,0:T(8,128)} %refs_1_.1, f32[1,128]{1,0:T(1,128)} %bitcast.20, ...), custom_call_target="tpu_custom_call" | custom-call | tf_op jit(solution)/shard_map/sweep/pallas_call | solution.py:575
  95.0 1.0 %copy.20 = f32[8,2,128,128]{3,2,1,0:T(8,128)} copy(f32[8,2,128,128]{3,2,1,0:T(8,128)S(1)} %bitcast.12) | data formatting | bytes 2097152
  96.0 1.0 copy.21
